TPU v7x, 768 devices: a whole 4x8x12 slice. The times are simulated.
768 devices in a mesh: row: 96 (over z, y_hi, core), col: 8 (over x, y_lo).
Axes of the slice: x: 4, y: 8 (y_hi: 4, y_lo: 2; y = y_hi * 2 + y_lo), z: 12, core: 2. Of those that a mesh axis runs over, the one named last changes fastest.
Arguments:
- features: bfloat16 [98304, 128], P(('row', 'col')), may hold values from -6 to 6
- tiles: bfloat16 [96, 8, 128, 128, 128], P('row', 'col'), may hold values from -0.0625 to 0.0625
- tile_index: int32 [96, 8, 128], P('row', 'col'), may hold values from 0 to 767, as said below
- tile_count: int32 [96, 8], P('row', 'col'), may hold values from 16 to 128, as said below
- w_first: bfloat16 [128, 256], replicated, may hold values from -0.5 to 0.5
- b_first: float32 [256], replicated, may hold values from -3 to 3
- w_second: bfloat16 [256, 128], replicated, may hold values from -0.375 to 0.375
- b_second: float32 [128], replicated, may hold values from -3 to 3
Outputs:
- logits: float32 [98304, 128], P(('row', 'col'))
Inputs may be any that keep to these rules, and one draw needn't show every extreme that they name: `tile_index`: within one device the live slots name distinct tiles. `tile_count`: some device has all 128 slots live; every count is 128 divided by 1, 2, 4 or 8.
All inputs are finite; a program needn't handle non-finite values.
Results may differ from a plain program's by a relative error of at most 0.01.
Values may be sent and summed in bfloat16 or wider, within the bound.
No kernel may reach another device: no remote copies, remote signals or barrier semaphores. Data moves between devices by JAX's collectives and lax.ppermute only.
A program may use at most 32 MiB of HBM per device.

v0:
```python
import functools

import jax
import jax.numpy as jnp
from jax import lax
from jax.experimental import pallas as pl
from jax.experimental.pallas import tpu as pltpu
from jax.sharding import Mesh, PartitionSpec as P

TILE = 128
ROW_TILES = 8
SLOTS = 128
CHUNKS = ((0, 16), (16, 16), (32, 32), (64, 32), (96, 32))
AXES = ("zq", "zt", "yh", "core", "x", "yl")
SIZES = (4, 3, 4, 2, 4, 2)
ROW = ("zq", "zt", "yh", "core")
COL = ("x", "yl")


def in_vmem(x):
    return pltpu.with_memory_space_constraint(x, pltpu.VMEM)


def spmm_kernel(count, rows, cols, tiles, *rest):
    pieces = rest[:6]
    out, tile_buf, feat, acc, tile_sems = rest[6:]
    live = count[0]

    def fetch(c):
        part = pl.ds(*CHUNKS[c])
        return pltpu.make_async_copy(tiles.at[part], tile_buf.at[part], tile_sems.at[c])

    def work(c):
        fetch(c).wait()
        start, size = CHUNKS[c]
        for u in range(start, start + size):
            acc[rows[u]] += jnp.dot(
                tile_buf[u], feat[cols[u]], preferred_element_type=jnp.float32
            )

    fetch(0).start()
    for c in range(1, len(CHUNKS)):
        pl.when(CHUNKS[c][0] < live)(fetch(c).start)

    acc[...] = jnp.zeros_like(acc)
    for p, piece in enumerate(pieces):
        feat[16 * p:16 * p + 16] = piece[...]
    work(0)
    for c in range(1, len(CHUNKS)):
        pl.when(CHUNKS[c][0] < live)(functools.partial(work, c))
    out[...] = acc[...].astype(out.dtype)


def spmm(count, rows, cols, tiles, pieces):
    smem = pl.BlockSpec(memory_space=pltpu.SMEM)
    vmem = pl.BlockSpec(memory_space=pltpu.VMEM)
    return pl.pallas_call(
        spmm_kernel,
        out_shape=jax.ShapeDtypeStruct((ROW_TILES, TILE, TILE), jnp.bfloat16),
        in_specs=[smem] * 3 + [pl.BlockSpec(memory_space=pl.ANY)] + [vmem] * 6,
        out_specs=vmem,
        scratch_shapes=[
            pltpu.VMEM((SLOTS, TILE, TILE), jnp.bfloat16),
            pltpu.VMEM((96, TILE, TILE), jnp.bfloat16),
            pltpu.VMEM((ROW_TILES, TILE, TILE), jnp.float32),
            pltpu.SemaphoreType.DMA((len(CHUNKS),)),
        ],
        compiler_params=pltpu.CompilerParams(vmem_limit_bytes=12 << 20),
        name="spmm",
    )(
        count,
        rows,
        cols,
        pltpu.with_memory_space_constraint(tiles, pltpu.HBM),
        *(in_vmem(piece) for piece in pieces),
    )


def dense_kernel(parts, w_first, b_first, w_second, out):
    total = jnp.sum(parts[...].astype(jnp.float32), axis=0).astype(jnp.bfloat16)
    hidden = jnp.dot(total, w_first[...], preferred_element_type=jnp.float32)
    hidden = jnp.maximum(hidden + b_first[...], 0.0).astype(jnp.bfloat16)
    projected = jnp.dot(hidden, w_second[...], preferred_element_type=jnp.float32)
    out[...] = jnp.broadcast_to(projected.astype(out.dtype)[None], out.shape)


def dense(parts, w_first, b_first, w_second):
    return pl.pallas_call(
        dense_kernel,
        out_shape=jax.ShapeDtypeStruct((4, TILE, TILE), jnp.bfloat16),
        in_specs=[pl.BlockSpec(memory_space=pltpu.VMEM)] * 4,
        out_specs=pl.BlockSpec(memory_space=pltpu.VMEM),
        compiler_params=pltpu.CompilerParams(vmem_limit_bytes=8 << 20),
        name="dense",
    )(*(in_vmem(x) for x in (parts, w_first, b_first[None], w_second)))


def gather(copies):
    column = lax.all_to_all(copies, "yh", 0, 0)
    own = lax.all_gather(column, "zq", axis=0).reshape(16, TILE, TILE)
    swap = [(0, 1), (1, 0)]
    left = lax.ppermute(own, ("zq", "zt"), [(k, (k + 1) % 12) for k in range(12)])
    right = lax.ppermute(own, ("zq", "zt"), [((k + 1) % 12, k) for k in range(12)])
    pieces = []
    for piece in (own, right, left):
        pieces += [piece, lax.ppermute(piece, "core", swap)]
    return pieces


def position(cols):
    core = lax.axis_index("core")
    third = lax.axis_index("zt")
    z = cols // 8
    side = (z % 3 + 3 - third) % 3
    other = jnp.where(cols % 2 == core, 0, 1)
    return (side * 2 + other) * 16 + z // 3 * 4 + cols // 2 % 4


def local(features, tiles, tile_index, tile_count, w_first, b_first, w_second, b_second):
    blocks = tiles[0, 0]
    index = tile_index[0, 0]
    count = tile_count[0]
    rows = index // 96
    cols = position(index % 96)

    def aggregate(copies):
        partial = spmm(count, rows, cols, blocks, gather(copies))
        return lax.all_to_all(partial, COL, 0, 0)

    first = aggregate(jnp.broadcast_to(features[None], (4, TILE, TILE)))
    second = aggregate(dense(first, w_first, b_first, w_second))
    return jnp.sum(second.astype(jnp.float32), axis=0) + b_second


def solution(mesh):
    fine = Mesh(mesh.devices.reshape(SIZES), AXES)
    in_specs = (
        P(ROW + COL, None),
        P(ROW, COL, None, None, None),
        P(ROW, COL, None),
        P(ROW, COL),
        P(),
        P(),
        P(),
        P(),
    )
    return jax.shard_map(
        local, mesh=fine, in_specs=in_specs, out_specs=P(ROW + COL, None), check_vma=False
    )
```

profile of v0, /device:TPU:1, one launch (start us, length us, event | category | flops | bytes accessed | tf_op | source)
XLA Modules:
  0.0 148.2 jit_solution(11573186510603659014)
XLA Ops:
  0.0 0.8 broadcast_in_dim.8
  0.8 14.8 %all_to_all.20 = bf16[4,128,128]{2,1,0:T(8,128)(2,1)S(1)} all-to-all(bf16[4,128,128]{2,1,0:T(8,128)(2,1)S(1)} %broadcast_in_dim.8), channel_id=1, replica_groups=mesh['zq'=4,'zt'=3,'yh'=4,'core'=2,'x'=4,'yl'=2] {'yh'}, dimensions={0} | all-to-all | bytes 262144 | tf_op jit(solution)/shard_map/all_to_all | solution.py:99
  15.6 26.3 %all-gather.rest_0_ = bf16[16,128,128]{2,1,0:T(8,128)(2,1)S(1)} all-gather(bf16[4,128,128]{2,1,0:T(8,128)(2,1)S(1)} %all_to_all.20), channel_id=2, replica_groups=mesh['zq'=4,'zt'=3,'yh'=4,'core'=2,'x'=4,'yl'=2] {'zq'}, dimensions={0}, use_global_device_ids=true | all-gather | bytes 655360 | tf_op jit(solution)/shard_map/all_gather | solution.py:100
  41.8 0.0 copy-start
  41.8 0.0 copy-start.1
  41.8 0.0 copy-start.2
  41.8 4.8 %collective-permute-start.3 = (bf16[16,128,128]{2,1,0:T(8,128)(2,1)S(1)}, bf16[16,128,128]{2,1,0:T(8,128)(2,1)S(1)}, u32[]{:S(2)}, u32[]{:S(2)}) collective-permute-start(bf16[16,128,128]{2,1,0:T(8,128)(2,1)S(1)} %all-gather.rest_0_), channel_id=1, source_target_pairs={{0,64},{64,128},{128,192},{192,256},{256,320},{320,384},{384,448},... | collective-permute-start | bytes 1572872 | tf_op jit(solution)/shard_map/ppermute | solution.py:102
  46.6 1.9 %collective-permute-start.1 = (bf16[16,128,128]{2,1,0:T(8,128)(2,1)S(1)}, bf16[16,128,128]{2,1,0:T(8,128)(2,1)S(1)}, u32[]{:S(2)}, u32[]{:S(2)}) collective-permute-start(bf16[16,128,128]{2,1,0:T(8,128)(2,1)S(1)} %all-gather.rest_0_), channel_id=1, source_target_pairs={{64,0},{128,64},{192,128},{256,192},{320,256},{384,320},{448,384},... | collective-permute-start | bytes 1572872 | tf_op jit(solution)/shard_map/ppermute | solution.py:103
  48.6 8.2 %collective-permute-start = (bf16[16,128,128]{2,1,0:T(8,128)(2,1)S(1)}, bf16[16,128,128]{2,1,0:T(8,128)(2,1)S(1)}, u32[]{:S(2)}, u32[]{:S(2)}) collective-permute-start(bf16[16,128,128]{2,1,0:T(8,128)(2,1)S(1)} %all-gather.rest_0_), channel_id=1, source_target_pairs={{0,8},{8,0},{1,9},{9,1},{2,10},{10,2},{3,11},{11,3},{4,12},{12,4},... | collective-permute-start | bytes 1572872 | tf_op jit(solution)/shard_map/ppermute | solution.py:106
  56.7 0.0 collective-permute-done.3.rest_4_
  56.7 5.2 %collective-permute-start.4 = (bf16[16,128,128]{2,1,0:T(8,128)(2,1)S(1)}, bf16[16,128,128]{2,1,0:T(8,128)(2,1)S(1)}, u32[]{:S(2)}, u32[]{:S(2)}) collective-permute-start(bf16[16,128,128]{2,1,0:T(8,128)(2,1)S(1)} %collective-permute-done.3.rest_4_), channel_id=1, source_target_pairs={{0,8},{8,0},{1,9},{9,1},{2,10},{10,2},{3,11},{11,3},{4,12},{12,4},... | collective-permute-start | bytes 1572872 | tf_op jit(solution)/shard_map/ppermute | solution.py:106
  61.9 0.0 collective-permute-done.1.rest_2_
  62.0 2.8 %collective-permute-start.2 = (bf16[16,128,128]{2,1,0:T(8,128)(2,1)S(1)}, bf16[16,128,128]{2,1,0:T(8,128)(2,1)S(1)}, u32[]{:S(2)}, u32[]{:S(2)}) collective-permute-start(bf16[16,128,128]{2,1,0:T(8,128)(2,1)S(1)} %collective-permute-done.1.rest_2_), channel_id=1, source_target_pairs={{0,8},{8,0},{1,9},{9,1},{2,10},{10,2},{3,11},{11,3},{4,12},{12,4},... | collective-permute-start | bytes 1572872 | tf_op jit(solution)/shard_map/ppermute | solution.py:106
  65.4 0.7 fusion.1
  66.1 0.0 collective-permute-done.rest_1_
  66.1 0.0 collective-permute-done.4.rest_5_
  66.1 0.1 collective-permute-done.2.rest_3_
  66.3 2.7 %spmm.2 = bf16[8,128,128]{2,1,0:T(8,128)(2,1)S(1)} custom-call(s32[1]{0:T(128)} %bitcast.14.count, s32[128]{0:T(128)S(1)} %get-tuple-element.6.rows, s32[128]{0:T(128)S(1)} %get-tuple-element.5.cols, bf16[128,128,128]{2,1,0:T(8,128)(2,1)} %bitcast.17, bf16[16,128,128]{2,1,0:T(8,128)(2,1)S(1)} %all-gather.rest_0_, ...), custom_call_target="tpu_custom_call" | custom-call | tf_op jit(solution)/shard_map/spmm/pallas_call | solution.py:57
  69.0 11.3 %all_to_all.21.parts = bf16[8,128,128]{2,1,0:T(8,128)(2,1)S(1)} all-to-all(bf16[8,128,128]{2,1,0:T(8,128)(2,1)S(1)} %spmm.2), channel_id=1, replica_groups=mesh['zq'=4,'zt'=3,'yh'=4,'core'=2,'x'=4,'yl'=2] {'x','yl'}, dimensions={0} | all-to-all | bytes 524288 | tf_op jit(solution)/shard_map/all_to_all | solution.py:128
  80.3 0.0 copy-done
  80.3 0.0 copy-done.1
  80.3 0.0 copy-done.2
  80.3 0.3 dense.1
  80.6 10.7 %all_to_all.22 = bf16[4,128,128]{2,1,0:T(8,128)(2,1)S(1)} all-to-all(bf16[4,128,128]{2,1,0:T(8,128)(2,1)S(1)} %dense.1), channel_id=1, replica_groups=mesh['zq'=4,'zt'=3,'yh'=4,'core'=2,'x'=4,'yl'=2] {'yh'}, dimensions={0} | all-to-all | bytes 262144 | tf_op jit(solution)/shard_map/all_to_all | solution.py:99
  91.3 20.1 %all-gather.1.rest_0_ = bf16[16,128,128]{2,1,0:T(8,128)(2,1)S(1)} all-gather(bf16[4,128,128]{2,1,0:T(8,128)(2,1)S(1)} %all_to_all.22), channel_id=3, replica_groups=mesh['zq'=4,'zt'=3,'yh'=4,'core'=2,'x'=4,'yl'=2] {'zq'}, dimensions={0}, use_global_device_ids=true | all-gather | bytes 655360 | tf_op jit(solution)/shard_map/all_gather | solution.py:100
  111.4 1.9 %collective-permute-start.8 = (bf16[16,128,128]{2,1,0:T(8,128)(2,1)S(1)}, bf16[16,128,128]{2,1,0:T(8,128)(2,1)S(1)}, u32[]{:S(2)}, u32[]{:S(2)}) collective-permute-start(bf16[16,128,128]{2,1,0:T(8,128)(2,1)S(1)} %all-gather.1.rest_0_), channel_id=1, source_target_pairs={{0,64},{64,128},{128,192},{192,256},{256,320},{320,384},{384,448},... | collective-permute-start | bytes 1572872 | tf_op jit(solution)/shard_map/ppermute | solution.py:102
  113.3 4.6 %collective-permute-start.6 = (bf16[16,128,128]{2,1,0:T(8,128)(2,1)S(1)}, bf16[16,128,128]{2,1,0:T(8,128)(2,1)S(1)}, u32[]{:S(2)}, u32[]{:S(2)}) collective-permute-start(bf16[16,128,128]{2,1,0:T(8,128)(2,1)S(1)} %all-gather.1.rest_0_), channel_id=1, source_target_pairs={{64,0},{128,64},{192,128},{256,192},{320,256},{384,320},{448,384},... | collective-permute-start | bytes 1572872 | tf_op jit(solution)/shard_map/ppermute | solution.py:103
  117.9 8.3 %collective-permute-start.5 = (bf16[16,128,128]{2,1,0:T(8,128)(2,1)S(1)}, bf16[16,128,128]{2,1,0:T(8,128)(2,1)S(1)}, u32[]{:S(2)}, u32[]{:S(2)}) collective-permute-start(bf16[16,128,128]{2,1,0:T(8,128)(2,1)S(1)} %all-gather.1.rest_0_), channel_id=1, source_target_pairs={{0,8},{8,0},{1,9},{9,1},{2,10},{10,2},{3,11},{11,3},{4,12},{12,4},... | collective-permute-start | bytes 1572872 | tf_op jit(solution)/shard_map/ppermute | solution.py:106
  126.3 0.0 collective-permute-done.8.rest_4_
  126.3 5.2 %collective-permute-start.9 = (bf16[16,128,128]{2,1,0:T(8,128)(2,1)S(1)}, bf16[16,128,128]{2,1,0:T(8,128)(2,1)S(1)}, u32[]{:S(2)}, u32[]{:S(2)}) collective-permute-start(bf16[16,128,128]{2,1,0:T(8,128)(2,1)S(1)} %collective-permute-done.8.rest_4_), channel_id=1, source_target_pairs={{0,8},{8,0},{1,9},{9,1},{2,10},{10,2},{3,11},{11,3},{4,12},{12,4},... | collective-permute-start | bytes 1572872 | tf_op jit(solution)/shard_map/ppermute | solution.py:106
  131.5 0.0 collective-permute-done.6.rest_2_
  131.5 1.9 %collective-permute-start.7 = (bf16[16,128,128]{2,1,0:T(8,128)(2,1)S(1)}, bf16[16,128,128]{2,1,0:T(8,128)(2,1)S(1)}, u32[]{:S(2)}, u32[]{:S(2)}) collective-permute-start(bf16[16,128,128]{2,1,0:T(8,128)(2,1)S(1)} %collective-permute-done.6.rest_2_), channel_id=1, source_target_pairs={{0,8},{8,0},{1,9},{9,1},{2,10},{10,2},{3,11},{11,3},{4,12},{12,4},... | collective-permute-start | bytes 1572872 | tf_op jit(solution)/shard_map/ppermute | solution.py:106
  133.4 0.0 collective-permute-done.5.rest_1_
  133.4 0.0 collective-permute-done.9.rest_5_
  133.4 1.9 %collective-permute-done.7.rest_3_ = bf16[16,128,128]{2,1,0:T(8,128)(2,1)S(1)} collective-permute-done((bf16[16,128,128]{2,1,0:T(8,128)(2,1)S(1)}, bf16[16,128,128]{2,1,0:T(8,128)(2,1)S(1)}, u32[]{:S(2)}, u32[]{:S(2)}) %collective-permute-start.7) | collective-permute-done | bytes 524320 | tf_op jit(solution)/shard_map/ppermute | solution.py:106
  135.3 0.0 copy-start.3
  135.3 2.7 %spmm.3 = bf16[8,128,128]{2,1,0:T(8,128)(2,1)S(1)} custom-call(s32[1]{0:T(128)} %bitcast.15.count, s32[128]{0:T(128)S(1)} %get-tuple-element.6.rows, s32[128]{0:T(128)S(1)} %get-tuple-element.5.cols, bf16[128,128,128]{2,1,0:T(8,128)(2,1)} %bitcast.18, bf16[16,128,128]{2,1,0:T(8,128)(2,1)S(1)} %all-gather.1.rest_0_, ...), custom_call_target="tpu_custom_call" | custom-call | tf_op jit(solution)/shard_map/spmm/pallas_call | solution.py:57
  138.0 9.5 %all_to_all.23 = bf16[8,128,128]{2,1,0:T(8,128)(2,1)S(1)} all-to-all(bf16[8,128,128]{2,1,0:T(8,128)(2,1)S(1)} %spmm.3), channel_id=1, replica_groups=mesh['zq'=4,'zt'=3,'yh'=4,'core'=2,'x'=4,'yl'=2] {'x','yl'}, dimensions={0} | all-to-all | bytes 524288 | tf_op jit(solution)/shard_map/all_to_all | solution.py:128
  147.5 0.0 copy-done.3
  147.5 0.6 broadcast_add_fusion
  (1 shorter events, 0.0 us)
Async XLA Ops:
  41.8 38.5 %copy-start = (bf16[128,256]{1,0:T(8,128)(2,1)S(1)}, bf16[128,256]{1,0:T(8,128)(2,1)}, u32[]{:S(2)}) copy-start(bf16[128,256]{1,0:T(8,128)(2,1)} %w_first.1) | copy-start | bytes 196612
  41.8 38.5 %copy-start.1 = (bf16[256,128]{1,0:T(8,128)(2,1)S(1)}, bf16[256,128]{1,0:T(8,128)(2,1)}, u32[]{:S(2)}) copy-start(bf16[256,128]{1,0:T(8,128)(2,1)} %w_second.1) | copy-start | bytes 196612
  41.8 38.5 %copy-start.2 = (f32[256]{0:T(256)S(1)}, f32[256]{0:T(256)}, u32[]{:S(2)}) copy-start(f32[256]{0:T(256)} %param.13) | copy-start | bytes 3076
  41.8 14.9 %collective-permute-start.3 = (bf16[16,128,128]{2,1,0:T(8,128)(2,1)S(1)}, bf16[16,128,128]{2,1,0:T(8,128)(2,1)S(1)}, u32[]{:S(2)}, u32[]{:S(2)}) collective-permute-start(bf16[16,128,128]{2,1,0:T(8,128)(2,1)S(1)} %all-gather.rest_0_), channel_id=1, source_target_pairs={{0,64},{64,128},{128,192},{192,256},{256,320},{320,384},{384,448},... | collective-permute-start | bytes 1572872 | tf_op jit(solution)/shard_map/ppermute | solution.py:102
  46.6 15.3 %collective-permute-start.1 = (bf16[16,128,128]{2,1,0:T(8,128)(2,1)S(1)}, bf16[16,128,128]{2,1,0:T(8,128)(2,1)S(1)}, u32[]{:S(2)}, u32[]{:S(2)}) collective-permute-start(bf16[16,128,128]{2,1,0:T(8,128)(2,1)S(1)} %all-gather.rest_0_), channel_id=1, source_target_pairs={{64,0},{128,64},{192,128},{256,192},{320,256},{384,320},{448,384},... | collective-permute-start | bytes 1572872 | tf_op jit(solution)/shard_map/ppermute | solution.py:103
  48.6 17.6 %collective-permute-start = (bf16[16,128,128]{2,1,0:T(8,128)(2,1)S(1)}, bf16[16,128,128]{2,1,0:T(8,128)(2,1)S(1)}, u32[]{:S(2)}, u32[]{:S(2)}) collective-permute-start(bf16[16,128,128]{2,1,0:T(8,128)(2,1)S(1)} %all-gather.rest_0_), channel_id=1, source_target_pairs={{0,8},{8,0},{1,9},{9,1},{2,10},{10,2},{3,11},{11,3},{4,12},{12,4},... | collective-permute-start | bytes 1572872 | tf_op jit(solution)/shard_map/ppermute | solution.py:106
  56.7 9.4 %collective-permute-start.4 = (bf16[16,128,128]{2,1,0:T(8,128)(2,1)S(1)}, bf16[16,128,128]{2,1,0:T(8,128)(2,1)S(1)}, u32[]{:S(2)}, u32[]{:S(2)}) collective-permute-start(bf16[16,128,128]{2,1,0:T(8,128)(2,1)S(1)} %collective-permute-done.3.rest_4_), channel_id=1, source_target_pairs={{0,8},{8,0},{1,9},{9,1},{2,10},{10,2},{3,11},{11,3},{4,12},{12,4},... | collective-permute-start | bytes 1572872 | tf_op jit(solution)/shard_map/ppermute | solution.py:106
  62.0 4.3 %collective-permute-start.2 = (bf16[16,128,128]{2,1,0:T(8,128)(2,1)S(1)}, bf16[16,128,128]{2,1,0:T(8,128)(2,1)S(1)}, u32[]{:S(2)}, u32[]{:S(2)}) collective-permute-start(bf16[16,128,128]{2,1,0:T(8,128)(2,1)S(1)} %collective-permute-done.1.rest_2_), channel_id=1, source_target_pairs={{0,8},{8,0},{1,9},{9,1},{2,10},{10,2},{3,11},{11,3},{4,12},{12,4},... | collective-permute-start | bytes 1572872 | tf_op jit(solution)/shard_map/ppermute | solution.py:106
  111.4 14.8 %collective-permute-start.8 = (bf16[16,128,128]{2,1,0:T(8,128)(2,1)S(1)}, bf16[16,128,128]{2,1,0:T(8,128)(2,1)S(1)}, u32[]{:S(2)}, u32[]{:S(2)}) collective-permute-start(bf16[16,128,128]{2,1,0:T(8,128)(2,1)S(1)} %all-gather.1.rest_0_), channel_id=1, source_target_pairs={{0,64},{64,128},{128,192},{192,256},{256,320},{320,384},{384,448},... | collective-permute-start | bytes 1572872 | tf_op jit(solution)/shard_map/ppermute | solution.py:102
  113.3 18.1 %collective-permute-start.6 = (bf16[16,128,128]{2,1,0:T(8,128)(2,1)S(1)}, bf16[16,128,128]{2,1,0:T(8,128)(2,1)S(1)}, u32[]{:S(2)}, u32[]{:S(2)}) collective-permute-start(bf16[16,128,128]{2,1,0:T(8,128)(2,1)S(1)} %all-gather.1.rest_0_), channel_id=1, source_target_pairs={{64,0},{128,64},{192,128},{256,192},{320,256},{384,320},{448,384},... | collective-permute-start | bytes 1572872 | tf_op jit(solution)/shard_map/ppermute | solution.py:103
  117.9 15.5 %collective-permute-start.5 = (bf16[16,128,128]{2,1,0:T(8,128)(2,1)S(1)}, bf16[16,128,128]{2,1,0:T(8,128)(2,1)S(1)}, u32[]{:S(2)}, u32[]{:S(2)}) collective-permute-start(bf16[16,128,128]{2,1,0:T(8,128)(2,1)S(1)} %all-gather.1.rest_0_), channel_id=1, source_target_pairs={{0,8},{8,0},{1,9},{9,1},{2,10},{10,2},{3,11},{11,3},{4,12},{12,4},... | collective-permute-start | bytes 1572872 | tf_op jit(solution)/shard_map/ppermute | solution.py:106
  126.3 7.1 %collective-permute-start.9 = (bf16[16,128,128]{2,1,0:T(8,128)(2,1)S(1)}, bf16[16,128,128]{2,1,0:T(8,128)(2,1)S(1)}, u32[]{:S(2)}, u32[]{:S(2)}) collective-permute-start(bf16[16,128,128]{2,1,0:T(8,128)(2,1)S(1)} %collective-permute-done.8.rest_4_), channel_id=1, source_target_pairs={{0,8},{8,0},{1,9},{9,1},{2,10},{10,2},{3,11},{11,3},{4,12},{12,4},... | collective-permute-start | bytes 1572872 | tf_op jit(solution)/shard_map/ppermute | solution.py:106
  131.5 3.8 %collective-permute-start.7 = (bf16[16,128,128]{2,1,0:T(8,128)(2,1)S(1)}, bf16[16,128,128]{2,1,0:T(8,128)(2,1)S(1)}, u32[]{:S(2)}, u32[]{:S(2)}) collective-permute-start(bf16[16,128,128]{2,1,0:T(8,128)(2,1)S(1)} %collective-permute-done.6.rest_2_), channel_id=1, source_target_pairs={{0,8},{8,0},{1,9},{9,1},{2,10},{10,2},{3,11},{11,3},{4,12},{12,4},... | collective-permute-start | bytes 1572872 | tf_op jit(solution)/shard_map/ppermute | solution.py:106
  135.3 12.3 %copy-start.3 = (f32[128]{0:T(128)S(1)}, f32[128]{0:T(128)}, u32[]{:S(2)}) copy-start(f32[128]{0:T(128)} %param.15) | copy-start | bytes 1540
where the time goes:
time: 149 us; the launch traced here: 148 us
  blocking collectives  92.6 us (62%)
  starting transfers between devices  44.8 us (30%)
  Pallas kernels  5.76 us (4%)
  waiting for transfers between devices  2.01 us (1%)
    all_gather x2, blocking collectives, gather(): own = lax.all_gather(column, 'zq', axis=0).reshape(16, TILE, TILE)  46.4 us
    ppermute x6, starting transfers between devices, gather(): pieces += [piece, lax.ppermute(piece, 'core', swap)]  31.6 us
    all_to_all x2, blocking collectives, gather(): column = lax.all_to_all(copies, 'yh', 0, 0)  25.5 us
    all_to_all x2, blocking collectives, aggregate(): return lax.all_to_all(partial, COL, 0, 0)  20.7 us
    ppermute x2, starting transfers between devices, gather(): lax.ppermute(own, ('zq', 'zt'), [(k, (k + 1) % 12) for k in range(12)])  6.69 us
    ppermute x2, starting transfers between devices, gather(): lax.ppermute(own, ('zq', 'zt'), [((k + 1) % 12, k) for k in range(12)])  6.49 us
    pallas_call x2, Pallas kernels, spmm(): pl.pallas_call(spmm_kernel, out_shape=jax.ShapeDtypeStruct((ROW_TILES, TI...  5.48 us
  transfers between devices with their start and end apart: 10, of which 2 were waited for; matrix products, arithmetic and copies ran while one was open for 0% of the time, Pallas kernels for 0%

commit v1 on v0

--- a/solution.py
+++ b/solution.py
@@ -99,10 +99,14 @@
     column = lax.all_to_all(copies, "yh", 0, 0)
     own = lax.all_gather(column, "zq", axis=0).reshape(16, TILE, TILE)
     swap = [(0, 1), (1, 0)]
-    left = lax.ppermute(own, ("zq", "zt"), [(k, (k + 1) % 12) for k in range(12)])
-    right = lax.ppermute(own, ("zq", "zt"), [((k + 1) % 12, k) for k in range(12)])
+    line = ("zq", "zt", "core")
+    crossed = []
+    for flip in range(2):
+        step = [1, -1] if flip == 0 else [-1, 1]
+        pairs = [(2 * z + c, (z + step[c]) % 12 * 2 + c) for z in range(12) for c in range(2)]
+        crossed.append(lax.ppermute(own, line, pairs))
     pieces = []
-    for piece in (own, right, left):
+    for piece in (own, *crossed):
         pieces += [piece, lax.ppermute(piece, "core", swap)]
     return pieces
 
@@ -111,9 +115,11 @@
     core = lax.axis_index("core")
     third = lax.axis_index("zt")
     z = cols // 8
+    source = cols % 2
     side = (z % 3 + 3 - third) % 3
-    other = jnp.where(cols % 2 == core, 0, 1)
-    return (side * 2 + other) * 16 + z // 3 * 4 + cols // 2 % 4
+    first = (side == 2) == (source == 0)
+    piece = jnp.where(side == 0, 0, jnp.where(first, 2, 4)) + jnp.where(source == core, 0, 1)
+    return piece * 16 + z // 3 * 4 + cols // 2 % 4
 
 
 def local(features, tiles, tile_index, tile_count, w_first, b_first, w_second, b_second):

time: 149 us -> 151 us (1.013)
  the two profiles are of different devices: /device:TPU:1 before, /device:TPU:16 now
where the time goes in v1:
time: 151 us
  blocking collectives  95.7 us (63%)
  starting transfers between devices  30.9 us (20%)
  waiting for transfers between devices  15.2 us (10%)
  Pallas kernels  5.77 us (4%)
    all_gather x2, blocking collectives, gather(): own = lax.all_gather(column, 'zq', axis=0).reshape(16, TILE, TILE)  43 us
    all_to_all x2, blocking collectives, gather(): column = lax.all_to_all(copies, 'yh', 0, 0)  28.1 us
    all_to_all x2, blocking collectives, aggregate(): return lax.all_to_all(partial, COL, 0, 0)  24.6 us
    ppermute x4, starting transfers between devices, gather(): crossed.append(lax.ppermute(own, line, pairs))  19.2 us
    ppermute x4, waiting for transfers between devices, gather(): crossed.append(lax.ppermute(own, line, pairs))  13 us
    ppermute x6, starting transfers between devices, gather(): pieces += [piece, lax.ppermute(piece, 'core', swap)]  11.6 us
    pallas_call x2, Pallas kernels, spmm(): pl.pallas_call(spmm_kernel, out_shape=jax.ShapeDtypeStruct((ROW_TILES, TI...  5.49 us
  transfers between devices with their start and end apart: 10, of which 6 were waited for; matrix products, arithmetic and copies ran while one was open for 0% of the time, Pallas kernels for 0%

profile of v1, /device:TPU:16, one launch (start us, length us, event | category | flops | bytes accessed | tf_op | source)
XLA Modules:
  0.0 150.5 jit_solution(6418836743169282531)
XLA Ops:
  0.0 0.8 broadcast_in_dim.21
  0.8 17.7 %all_to_all.20 = bf16[4,128,128]{2,1,0:T(8,128)(2,1)S(1)} all-to-all(bf16[4,128,128]{2,1,0:T(8,128)(2,1)S(1)} %broadcast_in_dim.21), channel_id=1, replica_groups=mesh['zq'=4,'zt'=3,'yh'=4,'core'=2,'x'=4,'yl'=2] {'yh'}, dimensions={0} | all-to-all | bytes 262144 | tf_op jit(solution)/shard_map/all_to_all | solution.py:99
  18.5 24.2 %all-gather.rest_0_ = bf16[16,128,128]{2,1,0:T(8,128)(2,1)S(1)} all-gather(bf16[4,128,128]{2,1,0:T(8,128)(2,1)S(1)} %all_to_all.20), channel_id=2, replica_groups=mesh['zq'=4,'zt'=3,'yh'=4,'core'=2,'x'=4,'yl'=2] {'zq'}, dimensions={0}, use_global_device_ids=true | all-gather | bytes 655360 | tf_op jit(solution)/shard_map/all_gather | solution.py:100
  42.7 0.0 copy-start
  42.7 0.0 copy-start.1
  42.7 0.0 copy-start.2
  42.8 7.1 %collective-permute-start.3 = (bf16[16,128,128]{2,1,0:T(8,128)(2,1)S(1)}, bf16[16,128,128]{2,1,0:T(8,128)(2,1)S(1)}, u32[]{:S(2)}, u32[]{:S(2)}) collective-permute-start(bf16[16,128,128]{2,1,0:T(8,128)(2,1)S(1)} %all-gather.rest_0_), channel_id=1, source_target_pairs={{0,704},{8,72},{64,0},{72,136},{128,64},{136,200},{192,128},{200,2... | collective-permute-start | bytes 1572872 | tf_op jit(solution)/shard_map/ppermute | solution.py:107
  49.8 1.9 %collective-permute-start.1 = (bf16[16,128,128]{2,1,0:T(8,128)(2,1)S(1)}, bf16[16,128,128]{2,1,0:T(8,128)(2,1)S(1)}, u32[]{:S(2)}, u32[]{:S(2)}) collective-permute-start(bf16[16,128,128]{2,1,0:T(8,128)(2,1)S(1)} %all-gather.rest_0_), channel_id=1, source_target_pairs={{0,64},{8,712},{64,128},{72,8},{128,192},{136,72},{192,256},{200,1... | collective-permute-start | bytes 1572872 | tf_op jit(solution)/shard_map/ppermute | solution.py:107
  51.7 1.9 %collective-permute-start = (bf16[16,128,128]{2,1,0:T(8,128)(2,1)S(1)}, bf16[16,128,128]{2,1,0:T(8,128)(2,1)S(1)}, u32[]{:S(2)}, u32[]{:S(2)}) collective-permute-start(bf16[16,128,128]{2,1,0:T(8,128)(2,1)S(1)} %all-gather.rest_0_), channel_id=1, source_target_pairs={{0,8},{8,0},{1,9},{9,1},{2,10},{10,2},{3,11},{11,3},{4,12},{12,4},... | collective-permute-start | bytes 1572872 | tf_op jit(solution)/shard_map/ppermute | solution.py:110
  53.7 6.2 %collective-permute-done.3.rest_4_ = bf16[16,128,128]{2,1,0:T(8,128)(2,1)S(1)} collective-permute-done((bf16[16,128,128]{2,1,0:T(8,128)(2,1)S(1)}, bf16[16,128,128]{2,1,0:T(8,128)(2,1)S(1)}, u32[]{:S(2)}, u32[]{:S(2)}) %collective-permute-start.3) | collective-permute-done | bytes 524320 | tf_op jit(solution)/shard_map/ppermute | solution.py:107
  59.8 1.9 %collective-permute-start.4 = (bf16[16,128,128]{2,1,0:T(8,128)(2,1)S(1)}, bf16[16,128,128]{2,1,0:T(8,128)(2,1)S(1)}, u32[]{:S(2)}, u32[]{:S(2)}) collective-permute-start(bf16[16,128,128]{2,1,0:T(8,128)(2,1)S(1)} %collective-permute-done.3.rest_4_), channel_id=1, source_target_pairs={{0,8},{8,0},{1,9},{9,1},{2,10},{10,2},{3,11},{11,3},{4,12},{12,4},... | collective-permute-start | bytes 1572872 | tf_op jit(solution)/shard_map/ppermute | solution.py:110
  61.7 0.4 collective-permute-done.1.rest_2_
  62.1 2.1 %collective-permute-start.2 = (bf16[16,128,128]{2,1,0:T(8,128)(2,1)S(1)}, bf16[16,128,128]{2,1,0:T(8,128)(2,1)S(1)}, u32[]{:S(2)}, u32[]{:S(2)}) collective-permute-start(bf16[16,128,128]{2,1,0:T(8,128)(2,1)S(1)} %collective-permute-done.1.rest_2_), channel_id=1, source_target_pairs={{0,8},{8,0},{1,9},{9,1},{2,10},{10,2},{3,11},{11,3},{4,12},{12,4},... | collective-permute-start | bytes 1572872 | tf_op jit(solution)/shard_map/ppermute | solution.py:110
  64.8 0.7 fusion.1
  65.5 0.0 collective-permute-done.rest_1_
  65.5 0.0 collective-permute-done.4.rest_5_
  65.5 0.3 collective-permute-done.2.rest_3_
  65.9 2.7 %spmm.2 = bf16[8,128,128]{2,1,0:T(8,128)(2,1)S(1)} custom-call(s32[1]{0:T(128)} %bitcast.14.count, s32[128]{0:T(128)S(1)} %get-tuple-element.6.rows, s32[128]{0:T(128)S(1)} %get-tuple-element.5.cols, bf16[128,128,128]{2,1,0:T(8,128)(2,1)} %bitcast.17, bf16[16,128,128]{2,1,0:T(8,128)(2,1)S(1)} %all-gather.rest_0_, ...), custom_call_target="tpu_custom_call" | custom-call | tf_op jit(solution)/shard_map/spmm/pallas_call | solution.py:57
  68.6 13.3 %all_to_all.21.parts = bf16[8,128,128]{2,1,0:T(8,128)(2,1)S(1)} all-to-all(bf16[8,128,128]{2,1,0:T(8,128)(2,1)S(1)} %spmm.2), channel_id=1, replica_groups=mesh['zq'=4,'zt'=3,'yh'=4,'core'=2,'x'=4,'yl'=2] {'x','yl'}, dimensions={0} | all-to-all | bytes 524288 | tf_op jit(solution)/shard_map/all_to_all | solution.py:134
  81.9 0.0 copy-done
  81.9 0.0 copy-done.1
  81.9 0.0 copy-done.2
  81.9 0.3 dense.1
  82.2 10.3 %all_to_all.22 = bf16[4,128,128]{2,1,0:T(8,128)(2,1)S(1)} all-to-all(bf16[4,128,128]{2,1,0:T(8,128)(2,1)S(1)} %dense.1), channel_id=1, replica_groups=mesh['zq'=4,'zt'=3,'yh'=4,'core'=2,'x'=4,'yl'=2] {'yh'}, dimensions={0} | all-to-all | bytes 262144 | tf_op jit(solution)/shard_map/all_to_all | solution.py:99
  92.5 18.8 %all-gather.1.rest_0_ = bf16[16,128,128]{2,1,0:T(8,128)(2,1)S(1)} all-gather(bf16[4,128,128]{2,1,0:T(8,128)(2,1)S(1)} %all_to_all.22), channel_id=3, replica_groups=mesh['zq'=4,'zt'=3,'yh'=4,'core'=2,'x'=4,'yl'=2] {'zq'}, dimensions={0}, use_global_device_ids=true | all-gather | bytes 655360 | tf_op jit(solution)/shard_map/all_gather | solution.py:100
  111.3 8.4 %collective-permute-start.8 = (bf16[16,128,128]{2,1,0:T(8,128)(2,1)S(1)}, bf16[16,128,128]{2,1,0:T(8,128)(2,1)S(1)}, u32[]{:S(2)}, u32[]{:S(2)}) collective-permute-start(bf16[16,128,128]{2,1,0:T(8,128)(2,1)S(1)} %all-gather.1.rest_0_), channel_id=1, source_target_pairs={{0,704},{8,72},{64,0},{72,136},{128,64},{136,200},{192,128},{200,2... | collective-permute-start | bytes 1572872 | tf_op jit(solution)/shard_map/ppermute | solution.py:107
  119.7 1.9 %collective-permute-start.6 = (bf16[16,128,128]{2,1,0:T(8,128)(2,1)S(1)}, bf16[16,128,128]{2,1,0:T(8,128)(2,1)S(1)}, u32[]{:S(2)}, u32[]{:S(2)}) collective-permute-start(bf16[16,128,128]{2,1,0:T(8,128)(2,1)S(1)} %all-gather.1.rest_0_), channel_id=1, source_target_pairs={{0,64},{8,712},{64,128},{72,8},{128,192},{136,72},{192,256},{200,1... | collective-permute-start | bytes 1572872 | tf_op jit(solution)/shard_map/ppermute | solution.py:107
  121.6 1.9 %collective-permute-start.5 = (bf16[16,128,128]{2,1,0:T(8,128)(2,1)S(1)}, bf16[16,128,128]{2,1,0:T(8,128)(2,1)S(1)}, u32[]{:S(2)}, u32[]{:S(2)}) collective-permute-start(bf16[16,128,128]{2,1,0:T(8,128)(2,1)S(1)} %all-gather.1.rest_0_), channel_id=1, source_target_pairs={{0,8},{8,0},{1,9},{9,1},{2,10},{10,2},{3,11},{11,3},{4,12},{12,4},... | collective-permute-start | bytes 1572872 | tf_op jit(solution)/shard_map/ppermute | solution.py:110
  123.5 5.3 %collective-permute-done.8.rest_4_ = bf16[16,128,128]{2,1,0:T(8,128)(2,1)S(1)} collective-permute-done((bf16[16,128,128]{2,1,0:T(8,128)(2,1)S(1)}, bf16[16,128,128]{2,1,0:T(8,128)(2,1)S(1)}, u32[]{:S(2)}, u32[]{:S(2)}) %collective-permute-start.8) | collective-permute-done | bytes 524320 | tf_op jit(solution)/shard_map/ppermute | solution.py:107
  128.9 1.9 %collective-permute-start.9 = (bf16[16,128,128]{2,1,0:T(8,128)(2,1)S(1)}, bf16[16,128,128]{2,1,0:T(8,128)(2,1)S(1)}, u32[]{:S(2)}, u32[]{:S(2)}) collective-permute-start(bf16[16,128,128]{2,1,0:T(8,128)(2,1)S(1)} %collective-permute-done.8.rest_4_), channel_id=1, source_target_pairs={{0,8},{8,0},{1,9},{9,1},{2,10},{10,2},{3,11},{11,3},{4,12},{12,4},... | collective-permute-start | bytes 1572872 | tf_op jit(solution)/shard_map/ppermute | solution.py:110
  130.8 1.2 collective-permute-done.6.rest_2_
  131.9 1.9 %collective-permute-start.7 = (bf16[16,128,128]{2,1,0:T(8,128)(2,1)S(1)}, bf16[16,128,128]{2,1,0:T(8,128)(2,1)S(1)}, u32[]{:S(2)}, u32[]{:S(2)}) collective-permute-start(bf16[16,128,128]{2,1,0:T(8,128)(2,1)S(1)} %collective-permute-done.6.rest_2_), channel_id=1, source_target_pairs={{0,8},{8,0},{1,9},{9,1},{2,10},{10,2},{3,11},{11,3},{4,12},{12,4},... | collective-permute-start | bytes 1572872 | tf_op jit(solution)/shard_map/ppermute | solution.py:110
  133.9 0.0 collective-permute-done.5.rest_1_
  133.9 0.0 collective-permute-done.9.rest_5_
  133.9 1.9 %collective-permute-done.7.rest_3_ = bf16[16,128,128]{2,1,0:T(8,128)(2,1)S(1)} collective-permute-done((bf16[16,128,128]{2,1,0:T(8,128)(2,1)S(1)}, bf16[16,128,128]{2,1,0:T(8,128)(2,1)S(1)}, u32[]{:S(2)}, u32[]{:S(2)}) %collective-permute-start.7) | collective-permute-done | bytes 524320 | tf_op jit(solution)/shard_map/ppermute | solution.py:110
  135.7 0.0 copy-start.3
  135.7 2.7 %spmm.3 = bf16[8,128,128]{2,1,0:T(8,128)(2,1)S(1)} custom-call(s32[1]{0:T(128)} %bitcast.15.count, s32[128]{0:T(128)S(1)} %get-tuple-element.6.rows, s32[128]{0:T(128)S(1)} %get-tuple-element.5.cols, bf16[128,128,128]{2,1,0:T(8,128)(2,1)} %bitcast.18, bf16[16,128,128]{2,1,0:T(8,128)(2,1)S(1)} %all-gather.1.rest_0_, ...), custom_call_target="tpu_custom_call" | custom-call | tf_op jit(solution)/shard_map/spmm/pallas_call | solution.py:57
  138.5 11.3 %all_to_all.23 = bf16[8,128,128]{2,1,0:T(8,128)(2,1)S(1)} all-to-all(bf16[8,128,128]{2,1,0:T(8,128)(2,1)S(1)} %spmm.3), channel_id=1, replica_groups=mesh['zq'=4,'zt'=3,'yh'=4,'core'=2,'x'=4,'yl'=2] {'x','yl'}, dimensions={0} | all-to-all | bytes 524288 | tf_op jit(solution)/shard_map/all_to_all | solution.py:134
  149.9 0.0 copy-done.3
  149.9 0.6 broadcast_add_fusion
  (1 shorter events, 0.0 us)
Async XLA Ops:
  42.7 39.2 %copy-start = (bf16[128,256]{1,0:T(8,128)(2,1)S(1)}, bf16[128,256]{1,0:T(8,128)(2,1)}, u32[]{:S(2)}) copy-start(bf16[128,256]{1,0:T(8,128)(2,1)} %w_first.1) | copy-start | bytes 196612
  42.7 39.2 %copy-start.1 = (bf16[256,128]{1,0:T(8,128)(2,1)S(1)}, bf16[256,128]{1,0:T(8,128)(2,1)}, u32[]{:S(2)}) copy-start(bf16[256,128]{1,0:T(8,128)(2,1)} %w_second.1) | copy-start | bytes 196612
  42.7 39.2 %copy-start.2 = (f32[256]{0:T(256)S(1)}, f32[256]{0:T(256)}, u32[]{:S(2)}) copy-start(f32[256]{0:T(256)} %param.13) | copy-start | bytes 3076
  42.8 17.1 %collective-permute-start.3 = (bf16[16,128,128]{2,1,0:T(8,128)(2,1)S(1)}, bf16[16,128,128]{2,1,0:T(8,128)(2,1)S(1)}, u32[]{:S(2)}, u32[]{:S(2)}) collective-permute-start(bf16[16,128,128]{2,1,0:T(8,128)(2,1)S(1)} %all-gather.rest_0_), channel_id=1, source_target_pairs={{0,704},{8,72},{64,0},{72,136},{128,64},{136,200},{192,128},{200,2... | collective-permute-start | bytes 1572872 | tf_op jit(solution)/shard_map/ppermute | solution.py:107
  49.8 12.3 %collective-permute-start.1 = (bf16[16,128,128]{2,1,0:T(8,128)(2,1)S(1)}, bf16[16,128,128]{2,1,0:T(8,128)(2,1)S(1)}, u32[]{:S(2)}, u32[]{:S(2)}) collective-permute-start(bf16[16,128,128]{2,1,0:T(8,128)(2,1)S(1)} %all-gather.rest_0_), channel_id=1, source_target_pairs={{0,64},{8,712},{64,128},{72,8},{128,192},{136,72},{192,256},{200,1... | collective-permute-start | bytes 1572872 | tf_op jit(solution)/shard_map/ppermute | solution.py:107
  51.7 13.8 %collective-permute-start = (bf16[16,128,128]{2,1,0:T(8,128)(2,1)S(1)}, bf16[16,128,128]{2,1,0:T(8,128)(2,1)S(1)}, u32[]{:S(2)}, u32[]{:S(2)}) collective-permute-start(bf16[16,128,128]{2,1,0:T(8,128)(2,1)S(1)} %all-gather.rest_0_), channel_id=1, source_target_pairs={{0,8},{8,0},{1,9},{9,1},{2,10},{10,2},{3,11},{11,3},{4,12},{12,4},... | collective-permute-start | bytes 1572872 | tf_op jit(solution)/shard_map/ppermute | solution.py:110
  59.8 5.7 %collective-permute-start.4 = (bf16[16,128,128]{2,1,0:T(8,128)(2,1)S(1)}, bf16[16,128,128]{2,1,0:T(8,128)(2,1)S(1)}, u32[]{:S(2)}, u32[]{:S(2)}) collective-permute-start(bf16[16,128,128]{2,1,0:T(8,128)(2,1)S(1)} %collective-permute-done.3.rest_4_), channel_id=1, source_target_pairs={{0,8},{8,0},{1,9},{9,1},{2,10},{10,2},{3,11},{11,3},{4,12},{12,4},... | collective-permute-start | bytes 1572872 | tf_op jit(solution)/shard_map/ppermute | solution.py:110
  62.1 3.8 %collective-permute-start.2 = (bf16[16,128,128]{2,1,0:T(8,128)(2,1)S(1)}, bf16[16,128,128]{2,1,0:T(8,128)(2,1)S(1)}, u32[]{:S(2)}, u32[]{:S(2)}) collective-permute-start(bf16[16,128,128]{2,1,0:T(8,128)(2,1)S(1)} %collective-permute-done.1.rest_2_), channel_id=1, source_target_pairs={{0,8},{8,0},{1,9},{9,1},{2,10},{10,2},{3,11},{11,3},{4,12},{12,4},... | collective-permute-start | bytes 1572872 | tf_op jit(solution)/shard_map/ppermute | solution.py:110
  111.3 17.6 %collective-permute-start.8 = (bf16[16,128,128]{2,1,0:T(8,128)(2,1)S(1)}, bf16[16,128,128]{2,1,0:T(8,128)(2,1)S(1)}, u32[]{:S(2)}, u32[]{:S(2)}) collective-permute-start(bf16[16,128,128]{2,1,0:T(8,128)(2,1)S(1)} %all-gather.1.rest_0_), channel_id=1, source_target_pairs={{0,704},{8,72},{64,0},{72,136},{128,64},{136,200},{192,128},{200,2... | collective-permute-start | bytes 1572872 | tf_op jit(solution)/shard_map/ppermute | solution.py:107
  119.7 12.3 %collective-permute-start.6 = (bf16[16,128,128]{2,1,0:T(8,128)(2,1)S(1)}, bf16[16,128,128]{2,1,0:T(8,128)(2,1)S(1)}, u32[]{:S(2)}, u32[]{:S(2)}) collective-permute-start(bf16[16,128,128]{2,1,0:T(8,128)(2,1)S(1)} %all-gather.1.rest_0_), channel_id=1, source_target_pairs={{0,64},{8,712},{64,128},{72,8},{128,192},{136,72},{192,256},{200,1... | collective-permute-start | bytes 1572872 | tf_op jit(solution)/shard_map/ppermute | solution.py:107
  121.6 12.3 %collective-permute-start.5 = (bf16[16,128,128]{2,1,0:T(8,128)(2,1)S(1)}, bf16[16,128,128]{2,1,0:T(8,128)(2,1)S(1)}, u32[]{:S(2)}, u32[]{:S(2)}) collective-permute-start(bf16[16,128,128]{2,1,0:T(8,128)(2,1)S(1)} %all-gather.1.rest_0_), channel_id=1, source_target_pairs={{0,8},{8,0},{1,9},{9,1},{2,10},{10,2},{3,11},{11,3},{4,12},{12,4},... | collective-permute-start | bytes 1572872 | tf_op jit(solution)/shard_map/ppermute | solution.py:110
  128.9 5.0 %collective-permute-start.9 = (bf16[16,128,128]{2,1,0:T(8,128)(2,1)S(1)}, bf16[16,128,128]{2,1,0:T(8,128)(2,1)S(1)}, u32[]{:S(2)}, u32[]{:S(2)}) collective-permute-start(bf16[16,128,128]{2,1,0:T(8,128)(2,1)S(1)} %collective-permute-done.8.rest_4_), channel_id=1, source_target_pairs={{0,8},{8,0},{1,9},{9,1},{2,10},{10,2},{3,11},{11,3},{4,12},{12,4},... | collective-permute-start | bytes 1572872 | tf_op jit(solution)/shard_map/ppermute | solution.py:110
  131.9 3.8 %collective-permute-start.7 = (bf16[16,128,128]{2,1,0:T(8,128)(2,1)S(1)}, bf16[16,128,128]{2,1,0:T(8,128)(2,1)S(1)}, u32[]{:S(2)}, u32[]{:S(2)}) collective-permute-start(bf16[16,128,128]{2,1,0:T(8,128)(2,1)S(1)} %collective-permute-done.6.rest_2_), channel_id=1, source_target_pairs={{0,8},{8,0},{1,9},{9,1},{2,10},{10,2},{3,11},{11,3},{4,12},{12,4},... | collective-permute-start | bytes 1572872 | tf_op jit(solution)/shard_map/ppermute | solution.py:110
  135.7 14.1 %copy-start.3 = (f32[128]{0:T(128)S(1)}, f32[128]{0:T(128)}, u32[]{:S(2)}) copy-start(f32[128]{0:T(128)} %param.15) | copy-start | bytes 1540

commit v2 on v0

--- a/solution.py
+++ b/solution.py
@@ -81,13 +81,13 @@
     hidden = jnp.dot(total, w_first[...], preferred_element_type=jnp.float32)
     hidden = jnp.maximum(hidden + b_first[...], 0.0).astype(jnp.bfloat16)
     projected = jnp.dot(hidden, w_second[...], preferred_element_type=jnp.float32)
-    out[...] = jnp.broadcast_to(projected.astype(out.dtype)[None], out.shape)
+    out[...] = projected.astype(out.dtype)
 
 
 def dense(parts, w_first, b_first, w_second):
     return pl.pallas_call(
         dense_kernel,
-        out_shape=jax.ShapeDtypeStruct((4, TILE, TILE), jnp.bfloat16),
+        out_shape=jax.ShapeDtypeStruct((TILE, TILE), jnp.bfloat16),
         in_specs=[pl.BlockSpec(memory_space=pltpu.VMEM)] * 4,
         out_specs=pl.BlockSpec(memory_space=pltpu.VMEM),
         compiler_params=pltpu.CompilerParams(vmem_limit_bytes=8 << 20),
@@ -95,8 +95,8 @@
     )(*(in_vmem(x) for x in (parts, w_first, b_first[None], w_second)))
 
 
-def gather(copies):
-    column = lax.all_to_all(copies, "yh", 0, 0)
+def gather(block):
+    column = lax.all_gather(block, "yh", axis=0)
     own = lax.all_gather(column, "zq", axis=0).reshape(16, TILE, TILE)
     swap = [(0, 1), (1, 0)]
     left = lax.ppermute(own, ("zq", "zt"), [(k, (k + 1) % 12) for k in range(12)])
@@ -123,11 +123,11 @@
     rows = index // 96
     cols = position(index % 96)
 
-    def aggregate(copies):
-        partial = spmm(count, rows, cols, blocks, gather(copies))
+    def aggregate(block):
+        partial = spmm(count, rows, cols, blocks, gather(block))
         return lax.all_to_all(partial, COL, 0, 0)
 
-    first = aggregate(jnp.broadcast_to(features[None], (4, TILE, TILE)))
+    first = aggregate(features)
     second = aggregate(dense(first, w_first, b_first, w_second))
     return jnp.sum(second.astype(jnp.float32), axis=0) + b_second
 

time: 149 us -> 148 us (level)
  starting transfers between devices: 44.8 us -> 49.2 us
  blocking collectives: 92.6 us -> 88.8 us
    all_gather x0 -> x2, blocking collectives: none -> 25.9 us  [gather(): column = lax.all_gather(block, 'yh', axis=0)]
    all_to_all x2 -> x0, blocking collectives: 25.5 us -> none  [gather(): column = lax.all_to_all(copies, 'yh', 0, 0)]
    ppermute x2, starting transfers between devices: 6.69 us -> 11.1 us  [gather(): lax.ppermute(own, ('zq', 'zt'), [(k, (k + 1) % 12) for k in range(12)])]
    all_gather x2, blocking collectives: 46.4 us -> 42.4 us  [gather(): own = lax.all_gather(column, 'zq', axis=0).reshape(16, TILE, TILE)]
where the time goes in v2:
time: 148 us
  blocking collectives  88.8 us (60%)
  starting transfers between devices  49.2 us (33%)
  Pallas kernels  5.76 us (4%)
  waiting for transfers between devices  1.65 us (1%)
    all_gather x2, blocking collectives, gather(): own = lax.all_gather(column, 'zq', axis=0).reshape(16, TILE, TILE)  42.4 us
    ppermute x6, starting transfers between devices, gather(): pieces += [piece, lax.ppermute(piece, 'core', swap)]  32.4 us
    all_gather x2, blocking collectives, gather(): column = lax.all_gather(block, 'yh', axis=0)  25.9 us
    all_to_all x2, blocking collectives, aggregate(): return lax.all_to_all(partial, COL, 0, 0)  20.5 us
    ppermute x2, starting transfers between devices, gather(): lax.ppermute(own, ('zq', 'zt'), [(k, (k + 1) % 12) for k in range(12)])  11.1 us
    ppermute x2, starting transfers between devices, gather(): lax.ppermute(own, ('zq', 'zt'), [((k + 1) % 12, k) for k in range(12)])  5.82 us
    pallas_call x2, Pallas kernels, spmm(): pl.pallas_call(spmm_kernel, out_shape=jax.ShapeDtypeStruct((ROW_TILES, TI...  5.48 us
  transfers between devices with their start and end apart: 10, of which 2 were waited for; matrix products, arithmetic and copies ran while one was open for 0% of the time, Pallas kernels for 0%

profile of v2, /device:TPU:1, one launch (start us, length us, event | category | flops | bytes accessed | tf_op | source)
XLA Modules:
  0.0 147.7 jit_solution(9461101940192791851)
XLA Ops:
  0.0 14.4 %all-gather = bf16[512,128]{1,0:T(8,128)(2,1)S(1)} all-gather(bf16[128,128]{1,0:T(8,128)(2,1)} %param.8), channel_id=2, replica_groups=mesh['zq'=4,'zt'=3,'yh'=4,'core'=2,'x'=4,'yl'=2] {'yh'}, dimensions={0}, use_global_device_ids=true | all-gather | bytes 163840 | tf_op jit(solution)/shard_map/all_gather | solution.py:99
  14.4 24.2 %all-gather.1.rest_0_ = bf16[16,128,128]{2,1,0:T(8,128)(2,1)S(1)} all-gather(bf16[4,128,128]{2,1,0:T(8,128)(2,1)S(1)} %bitcast.22), channel_id=3, replica_groups=mesh['zq'=4,'zt'=3,'yh'=4,'core'=2,'x'=4,'yl'=2] {'zq'}, dimensions={0}, use_global_device_ids=true | all-gather | bytes 655360 | tf_op jit(solution)/shard_map/all_gather | solution.py:100
  38.6 0.0 copy-start
  38.6 0.0 copy-start.1
  38.6 0.0 copy-start.2
  38.6 5.9 %collective-permute-start.3 = (bf16[16,128,128]{2,1,0:T(8,128)(2,1)S(1)}, bf16[16,128,128]{2,1,0:T(8,128)(2,1)S(1)}, u32[]{:S(2)}, u32[]{:S(2)}) collective-permute-start(bf16[16,128,128]{2,1,0:T(8,128)(2,1)S(1)} %all-gather.1.rest_0_), channel_id=1, source_target_pairs={{0,64},{64,128},{128,192},{192,256},{256,320},{320,384},{384,448},... | collective-permute-start | bytes 1572872 | tf_op jit(solution)/shard_map/ppermute | solution.py:102
  44.6 3.9 %collective-permute-start.1 = (bf16[16,128,128]{2,1,0:T(8,128)(2,1)S(1)}, bf16[16,128,128]{2,1,0:T(8,128)(2,1)S(1)}, u32[]{:S(2)}, u32[]{:S(2)}) collective-permute-start(bf16[16,128,128]{2,1,0:T(8,128)(2,1)S(1)} %all-gather.1.rest_0_), channel_id=1, source_target_pairs={{64,0},{128,64},{192,128},{256,192},{320,256},{384,320},{448,384},... | collective-permute-start | bytes 1572872 | tf_op jit(solution)/shard_map/ppermute | solution.py:103
  48.5 7.4 %collective-permute-start = (bf16[16,128,128]{2,1,0:T(8,128)(2,1)S(1)}, bf16[16,128,128]{2,1,0:T(8,128)(2,1)S(1)}, u32[]{:S(2)}, u32[]{:S(2)}) collective-permute-start(bf16[16,128,128]{2,1,0:T(8,128)(2,1)S(1)} %all-gather.1.rest_0_), channel_id=1, source_target_pairs={{0,8},{8,0},{1,9},{9,1},{2,10},{10,2},{3,11},{11,3},{4,12},{12,4},... | collective-permute-start | bytes 1572872 | tf_op jit(solution)/shard_map/ppermute | solution.py:106
  55.9 0.0 collective-permute-done.3.rest_4_
  55.9 5.4 %collective-permute-start.4 = (bf16[16,128,128]{2,1,0:T(8,128)(2,1)S(1)}, bf16[16,128,128]{2,1,0:T(8,128)(2,1)S(1)}, u32[]{:S(2)}, u32[]{:S(2)}) collective-permute-start(bf16[16,128,128]{2,1,0:T(8,128)(2,1)S(1)} %collective-permute-done.3.rest_4_), channel_id=1, source_target_pairs={{0,8},{8,0},{1,9},{9,1},{2,10},{10,2},{3,11},{11,3},{4,12},{12,4},... | collective-permute-start | bytes 1572872 | tf_op jit(solution)/shard_map/ppermute | solution.py:106
  61.3 0.0 collective-permute-done.1.rest_2_
  61.3 2.4 %collective-permute-start.2 = (bf16[16,128,128]{2,1,0:T(8,128)(2,1)S(1)}, bf16[16,128,128]{2,1,0:T(8,128)(2,1)S(1)}, u32[]{:S(2)}, u32[]{:S(2)}) collective-permute-start(bf16[16,128,128]{2,1,0:T(8,128)(2,1)S(1)} %collective-permute-done.1.rest_2_), channel_id=1, source_target_pairs={{0,8},{8,0},{1,9},{9,1},{2,10},{10,2},{3,11},{11,3},{4,12},{12,4},... | collective-permute-start | bytes 1572872 | tf_op jit(solution)/shard_map/ppermute | solution.py:106
  64.3 0.7 fusion.1
  65.0 0.0 collective-permute-done.rest_1_
  65.1 0.0 collective-permute-done.4.rest_5_
  65.1 0.1 collective-permute-done.2.rest_3_
  65.2 2.7 %spmm.2 = bf16[8,128,128]{2,1,0:T(8,128)(2,1)S(1)} custom-call(s32[1]{0:T(128)} %bitcast.16.count, s32[128]{0:T(128)S(1)} %get-tuple-element.6.rows, s32[128]{0:T(128)S(1)} %get-tuple-element.5.cols, bf16[128,128,128]{2,1,0:T(8,128)(2,1)} %bitcast.19, bf16[16,128,128]{2,1,0:T(8,128)(2,1)S(1)} %all-gather.1.rest_0_, ...), custom_call_target="tpu_custom_call" | custom-call | tf_op jit(solution)/shard_map/spmm/pallas_call | solution.py:57
  67.9 11.4 %all_to_all.10.parts = bf16[8,128,128]{2,1,0:T(8,128)(2,1)S(1)} all-to-all(bf16[8,128,128]{2,1,0:T(8,128)(2,1)S(1)} %spmm.2), channel_id=1, replica_groups=mesh['zq'=4,'zt'=3,'yh'=4,'core'=2,'x'=4,'yl'=2] {'x','yl'}, dimensions={0} | all-to-all | bytes 524288 | tf_op jit(solution)/shard_map/all_to_all | solution.py:128
  79.3 0.0 copy-done
  79.3 0.0 copy-done.1
  79.3 0.0 copy-done.2
  79.3 0.3 dense.1
  79.6 11.5 %all-gather.2 = bf16[512,128]{1,0:T(8,128)(2,1)S(1)} all-gather(bf16[128,128]{1,0:T(8,128)(2,1)S(1)} %dense.1), channel_id=4, replica_groups=mesh['zq'=4,'zt'=3,'yh'=4,'core'=2,'x'=4,'yl'=2] {'yh'}, dimensions={0}, use_global_device_ids=true | all-gather | bytes 163840 | tf_op jit(solution)/shard_map/all_gather | solution.py:99
  91.1 18.1 %all-gather.3.rest_0_ = bf16[16,128,128]{2,1,0:T(8,128)(2,1)S(1)} all-gather(bf16[4,128,128]{2,1,0:T(8,128)(2,1)S(1)} %bitcast.21), channel_id=5, replica_groups=mesh['zq'=4,'zt'=3,'yh'=4,'core'=2,'x'=4,'yl'=2] {'zq'}, dimensions={0}, use_global_device_ids=true | all-gather | bytes 655360 | tf_op jit(solution)/shard_map/all_gather | solution.py:100
  109.3 5.1 %collective-permute-start.8 = (bf16[16,128,128]{2,1,0:T(8,128)(2,1)S(1)}, bf16[16,128,128]{2,1,0:T(8,128)(2,1)S(1)}, u32[]{:S(2)}, u32[]{:S(2)}) collective-permute-start(bf16[16,128,128]{2,1,0:T(8,128)(2,1)S(1)} %all-gather.3.rest_0_), channel_id=1, source_target_pairs={{0,64},{64,128},{128,192},{192,256},{256,320},{320,384},{384,448},... | collective-permute-start | bytes 1572872 | tf_op jit(solution)/shard_map/ppermute | solution.py:102
  114.4 1.9 %collective-permute-start.6 = (bf16[16,128,128]{2,1,0:T(8,128)(2,1)S(1)}, bf16[16,128,128]{2,1,0:T(8,128)(2,1)S(1)}, u32[]{:S(2)}, u32[]{:S(2)}) collective-permute-start(bf16[16,128,128]{2,1,0:T(8,128)(2,1)S(1)} %all-gather.3.rest_0_), channel_id=1, source_target_pairs={{64,0},{128,64},{192,128},{256,192},{320,256},{384,320},{448,384},... | collective-permute-start | bytes 1572872 | tf_op jit(solution)/shard_map/ppermute | solution.py:103
  116.4 9.6 %collective-permute-start.5 = (bf16[16,128,128]{2,1,0:T(8,128)(2,1)S(1)}, bf16[16,128,128]{2,1,0:T(8,128)(2,1)S(1)}, u32[]{:S(2)}, u32[]{:S(2)}) collective-permute-start(bf16[16,128,128]{2,1,0:T(8,128)(2,1)S(1)} %all-gather.3.rest_0_), channel_id=1, source_target_pairs={{0,8},{8,0},{1,9},{9,1},{2,10},{10,2},{3,11},{11,3},{4,12},{12,4},... | collective-permute-start | bytes 1572872 | tf_op jit(solution)/shard_map/ppermute | solution.py:106
  126.0 0.0 collective-permute-done.8.rest_4_
  126.0 5.2 %collective-permute-start.9 = (bf16[16,128,128]{2,1,0:T(8,128)(2,1)S(1)}, bf16[16,128,128]{2,1,0:T(8,128)(2,1)S(1)}, u32[]{:S(2)}, u32[]{:S(2)}) collective-permute-start(bf16[16,128,128]{2,1,0:T(8,128)(2,1)S(1)} %collective-permute-done.8.rest_4_), channel_id=1, source_target_pairs={{0,8},{8,0},{1,9},{9,1},{2,10},{10,2},{3,11},{11,3},{4,12},{12,4},... | collective-permute-start | bytes 1572872 | tf_op jit(solution)/shard_map/ppermute | solution.py:106
  131.2 0.0 collective-permute-done.6.rest_2_
  131.2 2.4 %collective-permute-start.7 = (bf16[16,128,128]{2,1,0:T(8,128)(2,1)S(1)}, bf16[16,128,128]{2,1,0:T(8,128)(2,1)S(1)}, u32[]{:S(2)}, u32[]{:S(2)}) collective-permute-start(bf16[16,128,128]{2,1,0:T(8,128)(2,1)S(1)} %collective-permute-done.6.rest_2_), channel_id=1, source_target_pairs={{0,8},{8,0},{1,9},{9,1},{2,10},{10,2},{3,11},{11,3},{4,12},{12,4},... | collective-permute-start | bytes 1572872 | tf_op jit(solution)/shard_map/ppermute | solution.py:106
  133.6 0.0 collective-permute-done.5.rest_1_
  133.6 0.0 collective-permute-done.9.rest_5_
  133.6 1.5 %collective-permute-done.7.rest_3_ = bf16[16,128,128]{2,1,0:T(8,128)(2,1)S(1)} collective-permute-done((bf16[16,128,128]{2,1,0:T(8,128)(2,1)S(1)}, bf16[16,128,128]{2,1,0:T(8,128)(2,1)S(1)}, u32[]{:S(2)}, u32[]{:S(2)}) %collective-permute-start.7) | collective-permute-done | bytes 524320 | tf_op jit(solution)/shard_map/ppermute | solution.py:106
  135.1 0.0 copy-start.3
  135.1 2.7 %spmm.3 = bf16[8,128,128]{2,1,0:T(8,128)(2,1)S(1)} custom-call(s32[1]{0:T(128)} %bitcast.17.count, s32[128]{0:T(128)S(1)} %get-tuple-element.6.rows, s32[128]{0:T(128)S(1)} %get-tuple-element.5.cols, bf16[128,128,128]{2,1,0:T(8,128)(2,1)} %bitcast.20, bf16[16,128,128]{2,1,0:T(8,128)(2,1)S(1)} %all-gather.3.rest_0_, ...), custom_call_target="tpu_custom_call" | custom-call | tf_op jit(solution)/shard_map/spmm/pallas_call | solution.py:57
  137.9 9.1 %all_to_all.11 = bf16[8,128,128]{2,1,0:T(8,128)(2,1)S(1)} all-to-all(bf16[8,128,128]{2,1,0:T(8,128)(2,1)S(1)} %spmm.3), channel_id=1, replica_groups=mesh['zq'=4,'zt'=3,'yh'=4,'core'=2,'x'=4,'yl'=2] {'x','yl'}, dimensions={0} | all-to-all | bytes 524288 | tf_op jit(solution)/shard_map/all_to_all | solution.py:128
  147.0 0.0 copy-done.3
  147.0 0.6 broadcast_add_fusion
  (1 shorter events, 0.0 us)
Async XLA Ops:
  38.6 40.7 %copy-start = (bf16[128,256]{1,0:T(8,128)(2,1)S(1)}, bf16[128,256]{1,0:T(8,128)(2,1)}, u32[]{:S(2)}) copy-start(bf16[128,256]{1,0:T(8,128)(2,1)} %w_first.1) | copy-start | bytes 196612
  38.6 40.7 %copy-start.1 = (bf16[256,128]{1,0:T(8,128)(2,1)S(1)}, bf16[256,128]{1,0:T(8,128)(2,1)}, u32[]{:S(2)}) copy-start(bf16[256,128]{1,0:T(8,128)(2,1)} %w_second.1) | copy-start | bytes 196612
  38.6 40.7 %copy-start.2 = (f32[256]{0:T(256)S(1)}, f32[256]{0:T(256)}, u32[]{:S(2)}) copy-start(f32[256]{0:T(256)} %param.13) | copy-start | bytes 3076
  38.6 17.2 %collective-permute-start.3 = (bf16[16,128,128]{2,1,0:T(8,128)(2,1)S(1)}, bf16[16,128,128]{2,1,0:T(8,128)(2,1)S(1)}, u32[]{:S(2)}, u32[]{:S(2)}) collective-permute-start(bf16[16,128,128]{2,1,0:T(8,128)(2,1)S(1)} %all-gather.1.rest_0_), channel_id=1, source_target_pairs={{0,64},{64,128},{128,192},{192,256},{256,320},{320,384},{384,448},... | collective-permute-start | bytes 1572872 | tf_op jit(solution)/shard_map/ppermute | solution.py:102
  44.6 16.8 %collective-permute-start.1 = (bf16[16,128,128]{2,1,0:T(8,128)(2,1)S(1)}, bf16[16,128,128]{2,1,0:T(8,128)(2,1)S(1)}, u32[]{:S(2)}, u32[]{:S(2)}) collective-permute-start(bf16[16,128,128]{2,1,0:T(8,128)(2,1)S(1)} %all-gather.1.rest_0_), channel_id=1, source_target_pairs={{64,0},{128,64},{192,128},{256,192},{320,256},{384,320},{448,384},... | collective-permute-start | bytes 1572872 | tf_op jit(solution)/shard_map/ppermute | solution.py:103
  48.5 16.6 %collective-permute-start = (bf16[16,128,128]{2,1,0:T(8,128)(2,1)S(1)}, bf16[16,128,128]{2,1,0:T(8,128)(2,1)S(1)}, u32[]{:S(2)}, u32[]{:S(2)}) collective-permute-start(bf16[16,128,128]{2,1,0:T(8,128)(2,1)S(1)} %all-gather.1.rest_0_), channel_id=1, source_target_pairs={{0,8},{8,0},{1,9},{9,1},{2,10},{10,2},{3,11},{11,3},{4,12},{12,4},... | collective-permute-start | bytes 1572872 | tf_op jit(solution)/shard_map/ppermute | solution.py:106
  55.9 9.2 %collective-permute-start.4 = (bf16[16,128,128]{2,1,0:T(8,128)(2,1)S(1)}, bf16[16,128,128]{2,1,0:T(8,128)(2,1)S(1)}, u32[]{:S(2)}, u32[]{:S(2)}) collective-permute-start(bf16[16,128,128]{2,1,0:T(8,128)(2,1)S(1)} %collective-permute-done.3.rest_4_), channel_id=1, source_target_pairs={{0,8},{8,0},{1,9},{9,1},{2,10},{10,2},{3,11},{11,3},{4,12},{12,4},... | collective-permute-start | bytes 1572872 | tf_op jit(solution)/shard_map/ppermute | solution.py:106
  61.3 3.9 %collective-permute-start.2 = (bf16[16,128,128]{2,1,0:T(8,128)(2,1)S(1)}, bf16[16,128,128]{2,1,0:T(8,128)(2,1)S(1)}, u32[]{:S(2)}, u32[]{:S(2)}) collective-permute-start(bf16[16,128,128]{2,1,0:T(8,128)(2,1)S(1)} %collective-permute-done.1.rest_2_), channel_id=1, source_target_pairs={{0,8},{8,0},{1,9},{9,1},{2,10},{10,2},{3,11},{11,3},{4,12},{12,4},... | collective-permute-start | bytes 1572872 | tf_op jit(solution)/shard_map/ppermute | solution.py:106
  109.3 16.7 %collective-permute-start.8 = (bf16[16,128,128]{2,1,0:T(8,128)(2,1)S(1)}, bf16[16,128,128]{2,1,0:T(8,128)(2,1)S(1)}, u32[]{:S(2)}, u32[]{:S(2)}) collective-permute-start(bf16[16,128,128]{2,1,0:T(8,128)(2,1)S(1)} %all-gather.3.rest_0_), channel_id=1, source_target_pairs={{0,64},{64,128},{128,192},{192,256},{256,320},{320,384},{384,448},... | collective-permute-start | bytes 1572872 | tf_op jit(solution)/shard_map/ppermute | solution.py:102
  114.4 16.8 %collective-permute-start.6 = (bf16[16,128,128]{2,1,0:T(8,128)(2,1)S(1)}, bf16[16,128,128]{2,1,0:T(8,128)(2,1)S(1)}, u32[]{:S(2)}, u32[]{:S(2)}) collective-permute-start(bf16[16,128,128]{2,1,0:T(8,128)(2,1)S(1)} %all-gather.3.rest_0_), channel_id=1, source_target_pairs={{64,0},{128,64},{192,128},{256,192},{320,256},{384,320},{448,384},... | collective-permute-start | bytes 1572872 | tf_op jit(solution)/shard_map/ppermute | solution.py:103
  116.4 17.2 %collective-permute-start.5 = (bf16[16,128,128]{2,1,0:T(8,128)(2,1)S(1)}, bf16[16,128,128]{2,1,0:T(8,128)(2,1)S(1)}, u32[]{:S(2)}, u32[]{:S(2)}) collective-permute-start(bf16[16,128,128]{2,1,0:T(8,128)(2,1)S(1)} %all-gather.3.rest_0_), channel_id=1, source_target_pairs={{0,8},{8,0},{1,9},{9,1},{2,10},{10,2},{3,11},{11,3},{4,12},{12,4},... | collective-permute-start | bytes 1572872 | tf_op jit(solution)/shard_map/ppermute | solution.py:106
  126.0 7.6 %collective-permute-start.9 = (bf16[16,128,128]{2,1,0:T(8,128)(2,1)S(1)}, bf16[16,128,128]{2,1,0:T(8,128)(2,1)S(1)}, u32[]{:S(2)}, u32[]{:S(2)}) collective-permute-start(bf16[16,128,128]{2,1,0:T(8,128)(2,1)S(1)} %collective-permute-done.8.rest_4_), channel_id=1, source_target_pairs={{0,8},{8,0},{1,9},{9,1},{2,10},{10,2},{3,11},{11,3},{4,12},{12,4},... | collective-permute-start | bytes 1572872 | tf_op jit(solution)/shard_map/ppermute | solution.py:106
  131.2 3.9 %collective-permute-start.7 = (bf16[16,128,128]{2,1,0:T(8,128)(2,1)S(1)}, bf16[16,128,128]{2,1,0:T(8,128)(2,1)S(1)}, u32[]{:S(2)}, u32[]{:S(2)}) collective-permute-start(bf16[16,128,128]{2,1,0:T(8,128)(2,1)S(1)} %collective-permute-done.6.rest_2_), channel_id=1, source_target_pairs={{0,8},{8,0},{1,9},{9,1},{2,10},{10,2},{3,11},{11,3},{4,12},{12,4},... | collective-permute-start | bytes 1572872 | tf_op jit(solution)/shard_map/ppermute | solution.py:106
  135.1 11.9 %copy-start.3 = (f32[128]{0:T(128)S(1)}, f32[128]{0:T(128)}, u32[]{:S(2)}) copy-start(f32[128]{0:T(128)} %param.15) | copy-start | bytes 1540

commit v3 on v2

--- a/solution.py
+++ b/solution.py
@@ -23,7 +23,7 @@
 
 def spmm_kernel(count, rows, cols, tiles, *rest):
     pieces = rest[:6]
-    out, tile_buf, feat, acc, tile_sems = rest[6:]
+    out, tile_buf, feat, *accs, tile_sems = rest[6:]
     live = count[0]
 
     def fetch(c):
@@ -34,7 +34,7 @@
         fetch(c).wait()
         start, size = CHUNKS[c]
         for u in range(start, start + size):
-            acc[rows[u]] += jnp.dot(
+            accs[u % 2][rows[u]] += jnp.dot(
                 tile_buf[u], feat[cols[u]], preferred_element_type=jnp.float32
             )
 
@@ -42,13 +42,14 @@
     for c in range(1, len(CHUNKS)):
         pl.when(CHUNKS[c][0] < live)(fetch(c).start)
 
-    acc[...] = jnp.zeros_like(acc)
+    for acc in accs:
+        acc[...] = jnp.zeros_like(acc)
     for p, piece in enumerate(pieces):
         feat[16 * p:16 * p + 16] = piece[...]
     work(0)
     for c in range(1, len(CHUNKS)):
         pl.when(CHUNKS[c][0] < live)(functools.partial(work, c))
-    out[...] = acc[...].astype(out.dtype)
+    out[...] = (accs[0][...] + accs[1][...]).astype(out.dtype)
 
 
 def spmm(count, rows, cols, tiles, pieces):
@@ -62,6 +63,7 @@
         scratch_shapes=[
             pltpu.VMEM((SLOTS, TILE, TILE), jnp.bfloat16),
             pltpu.VMEM((96, TILE, TILE), jnp.bfloat16),
+            pltpu.VMEM((ROW_TILES, TILE, TILE), jnp.float32),
             pltpu.VMEM((ROW_TILES, TILE, TILE), jnp.float32),
             pltpu.SemaphoreType.DMA((len(CHUNKS),)),
         ],
@@ -96,8 +98,8 @@
 
 
 def gather(block):
-    column = lax.all_gather(block, "yh", axis=0)
-    own = lax.all_gather(column, "zq", axis=0).reshape(16, TILE, TILE)
+    column = lax.all_gather(block, "yh", axis=0, tiled=True)
+    own = lax.all_gather(column, "zq", axis=0, tiled=True).reshape(16, TILE, TILE)
     swap = [(0, 1), (1, 0)]
     left = lax.ppermute(own, ("zq", "zt"), [(k, (k + 1) % 12) for k in range(12)])
     right = lax.ppermute(own, ("zq", "zt"), [((k + 1) % 12, k) for k in range(12)])

time: 148 us -> 148 us (level)
  no operation moved by 1% of the time
where the time goes in v3:
time: 148 us; the launch traced here: 147 us
  blocking collectives  88 us (59%)
  starting transfers between devices  49.3 us (33%)
  Pallas kernels  5.78 us (4%)
  waiting for transfers between devices  1.67 us (1%)
    all_gather x2, blocking collectives, gather(): lax.all_gather(column, 'zq', axis=0, tiled=True).reshape(16, TILE, TILE)  42.1 us
    ppermute x6, starting transfers between devices, gather(): pieces += [piece, lax.ppermute(piece, 'core', swap)]  32.5 us
    all_gather x2, blocking collectives, gather(): column = lax.all_gather(block, 'yh', axis=0, tiled=True)  25.9 us
    all_to_all x2, blocking collectives, aggregate(): return lax.all_to_all(partial, COL, 0, 0)  20 us
    ppermute x2, starting transfers between devices, gather(): lax.ppermute(own, ('zq', 'zt'), [(k, (k + 1) % 12) for k in range(12)])  11 us
    ppermute x2, starting transfers between devices, gather(): lax.ppermute(own, ('zq', 'zt'), [((k + 1) % 12, k) for k in range(12)])  5.82 us
    pallas_call x2, Pallas kernels, spmm(): pl.pallas_call(spmm_kernel, out_shape=jax.ShapeDtypeStruct((ROW_TILES, TI...  5.49 us
  transfers between devices with their start and end apart: 10, of which 2 were waited for; matrix products, arithmetic and copies ran while one was open for 0% of the time, Pallas kernels for 0%

profile of v3, /device:TPU:1, one launch (start us, length us, event | category | flops | bytes accessed | tf_op | source)
XLA Modules:
  0.0 147.0 jit_solution(17685898207391229666)
XLA Ops:
  0.0 14.4 %all_gather.12 = bf16[512,128]{1,0:T(8,128)(2,1)S(1)} all-gather(bf16[128,128]{1,0:T(8,128)(2,1)} %param.8), channel_id=1, replica_groups=mesh['zq'=4,'zt'=3,'yh'=4,'core'=2,'x'=4,'yl'=2] {'yh'}, dimensions={0}, use_global_device_ids=true | all-gather | bytes 163840 | tf_op jit(solution)/shard_map/all_gather | solution.py:101
  14.4 24.2 %all_gather.13 = bf16[2048,128]{1,0:T(8,128)(2,1)S(1)} all-gather(bf16[512,128]{1,0:T(8,128)(2,1)S(1)} %all_gather.12), channel_id=1, replica_groups=mesh['zq'=4,'zt'=3,'yh'=4,'core'=2,'x'=4,'yl'=2] {'zq'}, dimensions={0}, use_global_device_ids=true | all-gather | bytes 655360 | tf_op jit(solution)/shard_map/all_gather | solution.py:102
  38.6 0.0 copy-start
  38.6 0.0 copy-start.1
  38.6 0.0 copy-start.2
  38.6 5.9 %collective-permute-start.3 = (bf16[16,128,128]{2,1,0:T(8,128)(2,1)S(1)}, bf16[16,128,128]{2,1,0:T(8,128)(2,1)S(1)}, u32[]{:S(2)}, u32[]{:S(2)}) collective-permute-start(bf16[16,128,128]{2,1,0:T(8,128)(2,1)S(1)} %bitcast.18), channel_id=1, source_target_pairs={{0,64},{64,128},{128,192},{192,256},{256,320},{320,384},{384,448},... | collective-permute-start | bytes 1572872 | tf_op jit(solution)/shard_map/ppermute | solution.py:104
  44.6 3.9 %collective-permute-start.1 = (bf16[16,128,128]{2,1,0:T(8,128)(2,1)S(1)}, bf16[16,128,128]{2,1,0:T(8,128)(2,1)S(1)}, u32[]{:S(2)}, u32[]{:S(2)}) collective-permute-start(bf16[16,128,128]{2,1,0:T(8,128)(2,1)S(1)} %bitcast.19), channel_id=1, source_target_pairs={{64,0},{128,64},{192,128},{256,192},{320,256},{384,320},{448,384},... | collective-permute-start | bytes 1572872 | tf_op jit(solution)/shard_map/ppermute | solution.py:105
  48.5 7.4 %collective-permute-start = (bf16[16,128,128]{2,1,0:T(8,128)(2,1)S(1)}, bf16[16,128,128]{2,1,0:T(8,128)(2,1)S(1)}, u32[]{:S(2)}, u32[]{:S(2)}) collective-permute-start(bf16[16,128,128]{2,1,0:T(8,128)(2,1)S(1)} %bitcast.20), channel_id=1, source_target_pairs={{0,8},{8,0},{1,9},{9,1},{2,10},{10,2},{3,11},{11,3},{4,12},{12,4},... | collective-permute-start | bytes 1572872 | tf_op jit(solution)/shard_map/ppermute | solution.py:108
  55.9 0.0 collective-permute-done.3.rest_4_
  55.9 5.4 %collective-permute-start.4 = (bf16[16,128,128]{2,1,0:T(8,128)(2,1)S(1)}, bf16[16,128,128]{2,1,0:T(8,128)(2,1)S(1)}, u32[]{:S(2)}, u32[]{:S(2)}) collective-permute-start(bf16[16,128,128]{2,1,0:T(8,128)(2,1)S(1)} %collective-permute-done.3.rest_4_), channel_id=1, source_target_pairs={{0,8},{8,0},{1,9},{9,1},{2,10},{10,2},{3,11},{11,3},{4,12},{12,4},... | collective-permute-start | bytes 1572872 | tf_op jit(solution)/shard_map/ppermute | solution.py:108
  61.3 0.0 collective-permute-done.1.rest_2_
  61.3 2.4 %collective-permute-start.2 = (bf16[16,128,128]{2,1,0:T(8,128)(2,1)S(1)}, bf16[16,128,128]{2,1,0:T(8,128)(2,1)S(1)}, u32[]{:S(2)}, u32[]{:S(2)}) collective-permute-start(bf16[16,128,128]{2,1,0:T(8,128)(2,1)S(1)} %collective-permute-done.1.rest_2_), channel_id=1, source_target_pairs={{0,8},{8,0},{1,9},{9,1},{2,10},{10,2},{3,11},{11,3},{4,12},{12,4},... | collective-permute-start | bytes 1572872 | tf_op jit(solution)/shard_map/ppermute | solution.py:108
  64.3 0.7 fusion.1
  65.0 0.0 collective-permute-done.rest_1_
  65.1 0.0 collective-permute-done.4.rest_5_
  65.1 0.1 collective-permute-done.2.rest_3_
  65.2 2.7 %spmm.2 = bf16[8,128,128]{2,1,0:T(8,128)(2,1)S(1)} custom-call(s32[1]{0:T(128)} %bitcast.16.count, s32[128]{0:T(128)S(1)} %get-tuple-element.6.rows, s32[128]{0:T(128)S(1)} %get-tuple-element.5.cols, bf16[128,128,128]{2,1,0:T(8,128)(2,1)} %bitcast.27, bf16[16,128,128]{2,1,0:T(8,128)(2,1)S(1)} %bitcast.21, ...), custom_call_target="tpu_custom_call" | custom-call | tf_op jit(solution)/shard_map/spmm/pallas_call | solution.py:58
  67.9 11.4 %all_to_all.10.parts = bf16[8,128,128]{2,1,0:T(8,128)(2,1)S(1)} all-to-all(bf16[8,128,128]{2,1,0:T(8,128)(2,1)S(1)} %spmm.2), channel_id=1, replica_groups=mesh['zq'=4,'zt'=3,'yh'=4,'core'=2,'x'=4,'yl'=2] {'x','yl'}, dimensions={0} | all-to-all | bytes 524288 | tf_op jit(solution)/shard_map/all_to_all | solution.py:130
  79.3 0.0 copy-done
  79.3 0.0 copy-done.1
  79.3 0.0 copy-done.2
  79.3 0.3 dense.1
  79.6 11.5 %all_gather.14 = bf16[512,128]{1,0:T(8,128)(2,1)S(1)} all-gather(bf16[128,128]{1,0:T(8,128)(2,1)S(1)} %dense.1), channel_id=1, replica_groups=mesh['zq'=4,'zt'=3,'yh'=4,'core'=2,'x'=4,'yl'=2] {'yh'}, dimensions={0}, use_global_device_ids=true | all-gather | bytes 163840 | tf_op jit(solution)/shard_map/all_gather | solution.py:101
  91.2 17.9 %all_gather.15 = bf16[2048,128]{1,0:T(8,128)(2,1)S(1)} all-gather(bf16[512,128]{1,0:T(8,128)(2,1)S(1)} %all_gather.14), channel_id=1, replica_groups=mesh['zq'=4,'zt'=3,'yh'=4,'core'=2,'x'=4,'yl'=2] {'zq'}, dimensions={0}, use_global_device_ids=true | all-gather | bytes 655360 | tf_op jit(solution)/shard_map/all_gather | solution.py:102
  109.1 5.1 %collective-permute-start.8 = (bf16[16,128,128]{2,1,0:T(8,128)(2,1)S(1)}, bf16[16,128,128]{2,1,0:T(8,128)(2,1)S(1)}, u32[]{:S(2)}, u32[]{:S(2)}) collective-permute-start(bf16[16,128,128]{2,1,0:T(8,128)(2,1)S(1)} %bitcast.22), channel_id=1, source_target_pairs={{0,64},{64,128},{128,192},{192,256},{256,320},{320,384},{384,448},... | collective-permute-start | bytes 1572872 | tf_op jit(solution)/shard_map/ppermute | solution.py:104
  114.2 1.9 %collective-permute-start.6 = (bf16[16,128,128]{2,1,0:T(8,128)(2,1)S(1)}, bf16[16,128,128]{2,1,0:T(8,128)(2,1)S(1)}, u32[]{:S(2)}, u32[]{:S(2)}) collective-permute-start(bf16[16,128,128]{2,1,0:T(8,128)(2,1)S(1)} %bitcast.23), channel_id=1, source_target_pairs={{64,0},{128,64},{192,128},{256,192},{320,256},{384,320},{448,384},... | collective-permute-start | bytes 1572872 | tf_op jit(solution)/shard_map/ppermute | solution.py:105
  116.1 9.8 %collective-permute-start.5 = (bf16[16,128,128]{2,1,0:T(8,128)(2,1)S(1)}, bf16[16,128,128]{2,1,0:T(8,128)(2,1)S(1)}, u32[]{:S(2)}, u32[]{:S(2)}) collective-permute-start(bf16[16,128,128]{2,1,0:T(8,128)(2,1)S(1)} %bitcast.24), channel_id=1, source_target_pairs={{0,8},{8,0},{1,9},{9,1},{2,10},{10,2},{3,11},{11,3},{4,12},{12,4},... | collective-permute-start | bytes 1572872 | tf_op jit(solution)/shard_map/ppermute | solution.py:108
  126.0 0.0 collective-permute-done.8.rest_4_
  126.0 5.2 %collective-permute-start.9 = (bf16[16,128,128]{2,1,0:T(8,128)(2,1)S(1)}, bf16[16,128,128]{2,1,0:T(8,128)(2,1)S(1)}, u32[]{:S(2)}, u32[]{:S(2)}) collective-permute-start(bf16[16,128,128]{2,1,0:T(8,128)(2,1)S(1)} %collective-permute-done.8.rest_4_), channel_id=1, source_target_pairs={{0,8},{8,0},{1,9},{9,1},{2,10},{10,2},{3,11},{11,3},{4,12},{12,4},... | collective-permute-start | bytes 1572872 | tf_op jit(solution)/shard_map/ppermute | solution.py:108
  131.2 0.0 collective-permute-done.6.rest_2_
  131.2 2.3 %collective-permute-start.7 = (bf16[16,128,128]{2,1,0:T(8,128)(2,1)S(1)}, bf16[16,128,128]{2,1,0:T(8,128)(2,1)S(1)}, u32[]{:S(2)}, u32[]{:S(2)}) collective-permute-start(bf16[16,128,128]{2,1,0:T(8,128)(2,1)S(1)} %collective-permute-done.6.rest_2_), channel_id=1, source_target_pairs={{0,8},{8,0},{1,9},{9,1},{2,10},{10,2},{3,11},{11,3},{4,12},{12,4},... | collective-permute-start | bytes 1572872 | tf_op jit(solution)/shard_map/ppermute | solution.py:108
  133.4 0.0 collective-permute-done.5.rest_1_
  133.5 0.0 collective-permute-done.9.rest_5_
  133.5 1.5 %collective-permute-done.7.rest_3_ = bf16[16,128,128]{2,1,0:T(8,128)(2,1)S(1)} collective-permute-done((bf16[16,128,128]{2,1,0:T(8,128)(2,1)S(1)}, bf16[16,128,128]{2,1,0:T(8,128)(2,1)S(1)}, u32[]{:S(2)}, u32[]{:S(2)}) %collective-permute-start.7) | collective-permute-done | bytes 524320 | tf_op jit(solution)/shard_map/ppermute | solution.py:108
  135.0 0.0 copy-start.3
  135.0 2.7 %spmm.3 = bf16[8,128,128]{2,1,0:T(8,128)(2,1)S(1)} custom-call(s32[1]{0:T(128)} %bitcast.17.count, s32[128]{0:T(128)S(1)} %get-tuple-element.6.rows, s32[128]{0:T(128)S(1)} %get-tuple-element.5.cols, bf16[128,128,128]{2,1,0:T(8,128)(2,1)} %bitcast.28, bf16[16,128,128]{2,1,0:T(8,128)(2,1)S(1)} %bitcast.25, ...), custom_call_target="tpu_custom_call" | custom-call | tf_op jit(solution)/shard_map/spmm/pallas_call | solution.py:58
  137.7 8.6 %all_to_all.11 = bf16[8,128,128]{2,1,0:T(8,128)(2,1)S(1)} all-to-all(bf16[8,128,128]{2,1,0:T(8,128)(2,1)S(1)} %spmm.3), channel_id=1, replica_groups=mesh['zq'=4,'zt'=3,'yh'=4,'core'=2,'x'=4,'yl'=2] {'x','yl'}, dimensions={0} | all-to-all | bytes 524288 | tf_op jit(solution)/shard_map/all_to_all | solution.py:130
  146.4 0.0 copy-done.3
  146.4 0.6 broadcast_add_fusion
  (1 shorter events, 0.0 us)
Async XLA Ops:
  38.6 40.7 %copy-start = (bf16[128,256]{1,0:T(8,128)(2,1)S(1)}, bf16[128,256]{1,0:T(8,128)(2,1)}, u32[]{:S(2)}) copy-start(bf16[128,256]{1,0:T(8,128)(2,1)} %w_first.1) | copy-start | bytes 196612
  38.6 40.7 %copy-start.1 = (bf16[256,128]{1,0:T(8,128)(2,1)S(1)}, bf16[256,128]{1,0:T(8,128)(2,1)}, u32[]{:S(2)}) copy-start(bf16[256,128]{1,0:T(8,128)(2,1)} %w_second.1) | copy-start | bytes 196612
  38.6 40.7 %copy-start.2 = (f32[256]{0:T(256)S(1)}, f32[256]{0:T(256)}, u32[]{:S(2)}) copy-start(f32[256]{0:T(256)} %param.13) | copy-start | bytes 3076
  38.6 17.2 %collective-permute-start.3 = (bf16[16,128,128]{2,1,0:T(8,128)(2,1)S(1)}, bf16[16,128,128]{2,1,0:T(8,128)(2,1)S(1)}, u32[]{:S(2)}, u32[]{:S(2)}) collective-permute-start(bf16[16,128,128]{2,1,0:T(8,128)(2,1)S(1)} %bitcast.18), channel_id=1, source_target_pairs={{0,64},{64,128},{128,192},{192,256},{256,320},{320,384},{384,448},... | collective-permute-start | bytes 1572872 | tf_op jit(solution)/shard_map/ppermute | solution.py:104
  44.6 16.8 %collective-permute-start.1 = (bf16[16,128,128]{2,1,0:T(8,128)(2,1)S(1)}, bf16[16,128,128]{2,1,0:T(8,128)(2,1)S(1)}, u32[]{:S(2)}, u32[]{:S(2)}) collective-permute-start(bf16[16,128,128]{2,1,0:T(8,128)(2,1)S(1)} %bitcast.19), channel_id=1, source_target_pairs={{64,0},{128,64},{192,128},{256,192},{320,256},{384,320},{448,384},... | collective-permute-start | bytes 1572872 | tf_op jit(solution)/shard_map/ppermute | solution.py:105
  48.5 16.6 %collective-permute-start = (bf16[16,128,128]{2,1,0:T(8,128)(2,1)S(1)}, bf16[16,128,128]{2,1,0:T(8,128)(2,1)S(1)}, u32[]{:S(2)}, u32[]{:S(2)}) collective-permute-start(bf16[16,128,128]{2,1,0:T(8,128)(2,1)S(1)} %bitcast.20), channel_id=1, source_target_pairs={{0,8},{8,0},{1,9},{9,1},{2,10},{10,2},{3,11},{11,3},{4,12},{12,4},... | collective-permute-start | bytes 1572872 | tf_op jit(solution)/shard_map/ppermute | solution.py:108
  55.9 9.2 %collective-permute-start.4 = (bf16[16,128,128]{2,1,0:T(8,128)(2,1)S(1)}, bf16[16,128,128]{2,1,0:T(8,128)(2,1)S(1)}, u32[]{:S(2)}, u32[]{:S(2)}) collective-permute-start(bf16[16,128,128]{2,1,0:T(8,128)(2,1)S(1)} %collective-permute-done.3.rest_4_), channel_id=1, source_target_pairs={{0,8},{8,0},{1,9},{9,1},{2,10},{10,2},{3,11},{11,3},{4,12},{12,4},... | collective-permute-start | bytes 1572872 | tf_op jit(solution)/shard_map/ppermute | solution.py:108
  61.3 3.9 %collective-permute-start.2 = (bf16[16,128,128]{2,1,0:T(8,128)(2,1)S(1)}, bf16[16,128,128]{2,1,0:T(8,128)(2,1)S(1)}, u32[]{:S(2)}, u32[]{:S(2)}) collective-permute-start(bf16[16,128,128]{2,1,0:T(8,128)(2,1)S(1)} %collective-permute-done.1.rest_2_), channel_id=1, source_target_pairs={{0,8},{8,0},{1,9},{9,1},{2,10},{10,2},{3,11},{11,3},{4,12},{12,4},... | collective-permute-start | bytes 1572872 | tf_op jit(solution)/shard_map/ppermute | solution.py:108
  109.1 16.9 %collective-permute-start.8 = (bf16[16,128,128]{2,1,0:T(8,128)(2,1)S(1)}, bf16[16,128,128]{2,1,0:T(8,128)(2,1)S(1)}, u32[]{:S(2)}, u32[]{:S(2)}) collective-permute-start(bf16[16,128,128]{2,1,0:T(8,128)(2,1)S(1)} %bitcast.22), channel_id=1, source_target_pairs={{0,64},{64,128},{128,192},{192,256},{256,320},{320,384},{384,448},... | collective-permute-start | bytes 1572872 | tf_op jit(solution)/shard_map/ppermute | solution.py:104
  114.2 17.0 %collective-permute-start.6 = (bf16[16,128,128]{2,1,0:T(8,128)(2,1)S(1)}, bf16[16,128,128]{2,1,0:T(8,128)(2,1)S(1)}, u32[]{:S(2)}, u32[]{:S(2)}) collective-permute-start(bf16[16,128,128]{2,1,0:T(8,128)(2,1)S(1)} %bitcast.23), channel_id=1, source_target_pairs={{64,0},{128,64},{192,128},{256,192},{320,256},{384,320},{448,384},... | collective-permute-start | bytes 1572872 | tf_op jit(solution)/shard_map/ppermute | solution.py:105
  116.1 17.3 %collective-permute-start.5 = (bf16[16,128,128]{2,1,0:T(8,128)(2,1)S(1)}, bf16[16,128,128]{2,1,0:T(8,128)(2,1)S(1)}, u32[]{:S(2)}, u32[]{:S(2)}) collective-permute-start(bf16[16,128,128]{2,1,0:T(8,128)(2,1)S(1)} %bitcast.24), channel_id=1, source_target_pairs={{0,8},{8,0},{1,9},{9,1},{2,10},{10,2},{3,11},{11,3},{4,12},{12,4},... | collective-permute-start | bytes 1572872 | tf_op jit(solution)/shard_map/ppermute | solution.py:108
  126.0 7.5 %collective-permute-start.9 = (bf16[16,128,128]{2,1,0:T(8,128)(2,1)S(1)}, bf16[16,128,128]{2,1,0:T(8,128)(2,1)S(1)}, u32[]{:S(2)}, u32[]{:S(2)}) collective-permute-start(bf16[16,128,128]{2,1,0:T(8,128)(2,1)S(1)} %collective-permute-done.8.rest_4_), channel_id=1, source_target_pairs={{0,8},{8,0},{1,9},{9,1},{2,10},{10,2},{3,11},{11,3},{4,12},{12,4},... | collective-permute-start | bytes 1572872 | tf_op jit(solution)/shard_map/ppermute | solution.py:108
  131.2 3.8 %collective-permute-start.7 = (bf16[16,128,128]{2,1,0:T(8,128)(2,1)S(1)}, bf16[16,128,128]{2,1,0:T(8,128)(2,1)S(1)}, u32[]{:S(2)}, u32[]{:S(2)}) collective-permute-start(bf16[16,128,128]{2,1,0:T(8,128)(2,1)S(1)} %collective-permute-done.6.rest_2_), channel_id=1, source_target_pairs={{0,8},{8,0},{1,9},{9,1},{2,10},{10,2},{3,11},{11,3},{4,12},{12,4},... | collective-permute-start | bytes 1572872 | tf_op jit(solution)/shard_map/ppermute | solution.py:108
  135.0 11.4 %copy-start.3 = (f32[128]{0:T(128)S(1)}, f32[128]{0:T(128)}, u32[]{:S(2)}) copy-start(f32[128]{0:T(128)} %param.15) | copy-start | bytes 1540
